TPU v7x, 512 devices: a whole 4x8x8 slice. The times are simulated.
512 devices in a mesh: row: 16 (over z_hi, y), col: 32 (over z_lo, x, core).
Axes of the slice: x: 4, y: 8, z: 8 (z_hi: 2, z_lo: 4; z = z_hi * 4 + z_lo), core: 2. Of those that a mesh axis runs over, the one named last changes fastest.
Arguments:
- amplitudes: bfloat16 [16384, 16384], P('row', 'col'), may hold values from -6 to 6
- aux_left: bfloat16 [16384, 1024], P('col', 'row'), may hold values from -0.046875 to 0.046875
- aux_right: bfloat16 [16384, 1024], P('col', 'row'), may hold values from -0.1875 to 0.1875
- occupied_map: int32 [16384], replicated, may hold values from 0 to 63
- virtual_map: int32 [16384], replicated, may hold values from 0 to 255
- occupied_energy: float32 [64], replicated, may hold values from -3 to -0.5
- virtual_energy: float32 [256], replicated, may hold values from 0.5 to 4
Outputs:
- residual_term: float32 [16384, 16384], P('row', 'col')
All inputs are finite; a program needn't handle non-finite values.
Results may differ from a plain program's by a relative error of at most 0.0029.
Values may be sent and summed in bfloat16 or wider, within the bound.
No kernel may reach another device: no remote copies, remote signals or barrier semaphores. Data moves between devices by JAX's collectives and lax.ppermute only.
A program may use at most 64 MiB of HBM per device.

v0:
```python
import itertools

import jax
import jax.numpy as jnp
from jax import lax
from jax.sharding import Mesh
from jax.sharding import PartitionSpec as P

ROW = ("zh", "y")
COL = ("zl", "x")
AUX_COL = ("x", "zl")
ALL = ("zh", "y", "zl", "x", "core")
SIZES = (2, 8, 4, 4, 2)
SWAP = [(0, 1), (1, 0)]
LEFT_SCALE = 2.0**20
RIGHT_SCALE = 2.0**18
FIT_SCALE = 8.0
SUM_SCALE = 128.0


def device_of(zh, y, zl, x, core):
    return (((zh * 8 + y) * 4 + zl) * 4 + x) * 2 + core


def chips(move, far=0):
    pairs = []
    for zh, y, zl, x, core in itertools.product(*(range(n) for n in SIZES)):
        to_zh, *rest = move(zh, y, zl, x)
        pairs.append((device_of(zh, y, zl, x, core), device_of(to_zh ^ far, *rest, core)))
    return pairs


def to_column(zh, y, zl, x):
    slot, block = x * 4 + zl, zh * 8 + y
    return slot & 1, slot >> 1, block // 4, block % 4


def to_row(zh, y, zl, x):
    slot, block = y * 2 + zh, zl * 4 + x
    return block // 8, block % 8, slot % 4, slot // 4


def pack(values, scale):
    return (values.astype(jnp.float32) * scale).astype(jnp.float16)


def restore(values, scale):
    return (values.astype(jnp.float32) * (1.0 / scale)).astype(jnp.bfloat16)


def lookup(positions, energy_table):
    matches = positions[:, None] == jnp.arange(energy_table.shape[0], dtype=jnp.int32)[None, :]
    return jnp.sum(jnp.where(matches, energy_table[None, :], 0.0), axis=1)


def pair_gap(occupied_map, virtual_map, occupied_energy, virtual_energy, offset, length):
    occupied_part = lax.dynamic_slice_in_dim(occupied_map, offset, length, 0)
    virtual_part = lax.dynamic_slice_in_dim(virtual_map, offset, length, 0)
    return lookup(virtual_part, virtual_energy) - lookup(occupied_part, occupied_energy)


def contract(left, right):
    return lax.dot_general(
        left, right, (((0,), (0,)), ((), ())), preferred_element_type=jnp.float32
    )


def per_device(
    amplitudes, aux_left, aux_right, occupied_map, virtual_map, occupied_energy, virtual_energy
):
    rows, cols = amplitudes.shape
    core = lax.axis_index("core")
    row_block = lax.axis_index(ROW)
    col_block = lax.axis_index(COL + ("core",))

    left = pack(aux_left.T, LEFT_SCALE)
    right = pack(aux_right.T, RIGHT_SCALE)
    near = lax.all_gather(jnp.concatenate([left, right], axis=0), ("zh", "core"), axis=0)
    near = near.reshape(2, 2, 2 * left.shape[0], cols)
    mine = lax.dynamic_index_in_dim(near, core, 1, keepdims=False)
    theirs = lax.dynamic_index_in_dim(near, 1 - core, 1, keepdims=False)
    chunk = jnp.concatenate(
        [
            lax.dynamic_slice_in_dim(mine, core * 32, 32, 1),
            lax.dynamic_slice_in_dim(theirs, core * 32, 32, 1),
            mine[:, 64:],
        ],
        axis=1,
    )
    factors = lax.all_gather(chunk, "y", axis=0, tiled=True)
    left_kept = restore(factors[:, :32], LEFT_SCALE).reshape(512, cols)
    left_taken = restore(factors[:, 32:64], LEFT_SCALE).reshape(512, cols)
    right_cols = restore(factors[:, 64:], RIGHT_SCALE).reshape(4, 4, 2, 32, cols)
    right_cols = right_cols.transpose(0, 2, 1, 3, 4).reshape(1024, cols)
    other_amplitudes = lax.ppermute(amplitudes, "core", SWAP)

    partial = lax.dot_general(
        left_kept, amplitudes, (((1,), (1,)), ((), ())), preferred_element_type=jnp.float32
    ) + lax.dot_general(
        left_taken, other_amplitudes, (((1,), (1,)), ((), ())), preferred_element_type=jnp.float32
    )
    sent = (partial * SUM_SCALE).astype(jnp.float16).reshape(16, 32, rows)
    right_moved = lax.ppermute(right, ALL, chips(to_row))
    arrived = lax.all_to_all(sent, AUX_COL, 0, 0)
    arrived, right_moved = lax.optimization_barrier((arrived, right_moved))
    summed = jnp.sum(arrived.astype(jnp.float32), axis=0) * (1.0 / SUM_SCALE)
    rounded = lax.reduce_precision(summed, exponent_bits=8, mantissa_bits=7)
    fitted = rounded.astype(jnp.bfloat16)
    light = (rounded * FIT_SCALE).astype(jnp.float16)
    light = jnp.concatenate([light[:, :cols], light[:, cols:]], axis=0)

    same = lax.ppermute(fitted, ALL, chips(to_column))
    cross = lax.ppermute(fitted, ALL, chips(to_column, 1))
    both = lax.all_gather(jnp.concatenate([right_moved, light], axis=0), "zl", axis=0)
    both, same, cross = lax.optimization_barrier((both, same, cross))
    both = both.reshape(2, 2, 4, 32, cols)
    right_part = both[:, :, :2].transpose(0, 2, 1, 3, 4).reshape(256, cols)
    fitted_part = both[:, :, 2:].transpose(2, 0, 1, 3, 4).reshape(256, cols)
    both = jnp.concatenate([right_part, fitted_part], axis=0)
    low = lax.axis_index("zh") == 0
    below, above = jnp.where(low, same, cross), jnp.where(low, cross, same)
    mirror_chunk = jnp.stack(
        [below[:, :cols], above[:, :cols], below[:, cols:], above[:, cols:]]
    )
    mirror = jnp.broadcast_to(mirror_chunk[None], (8,) + mirror_chunk.shape)
    mirror = lax.all_to_all(mirror.reshape(16, 2, 32, cols), ("y", "core"), 0, 0)
    both = lax.all_gather(both, ("x", "core"), axis=0).reshape(4, 2, 512, cols)
    mirror = mirror.reshape(1024, cols)

    halves = []
    for half in range(2):
        right_rows = restore(both[:, half, :256], RIGHT_SCALE).reshape(1024, cols)
        start = 256 + half * 128
        fitted_rows = restore(both[:, :, start : start + 128], FIT_SCALE).reshape(1024, cols)
        halves.append(contract(fitted_rows, right_cols) + contract(right_rows, mirror))
    total = jnp.concatenate(halves, axis=0)
    row_gap = pair_gap(
        occupied_map, virtual_map, occupied_energy, virtual_energy, row_block * rows, rows
    )
    col_gap = pair_gap(
        occupied_map, virtual_map, occupied_energy, virtual_energy, col_block * cols, cols
    )
    return total / (row_gap[:, None] + col_gap[None, :])


def solution(mesh):
    fine = Mesh(mesh.devices.reshape(SIZES), ALL)
    by_block = P(ROW, COL + ("core",))
    by_aux = P(COL + ("core",), ROW)
    return jax.shard_map(
        per_device,
        mesh=fine,
        in_specs=(by_block, by_aux, by_aux, P(), P(), P(), P()),
        out_specs=by_block,
        check_vma=False,
    )
```

profile of v0, /device:TPU:1, one launch (start us, length us, event | category | flops | bytes accessed | tf_op | source)
XLA Modules:
  0.0 163.7 jit_solution(16005404916720935738)
XLA Ops:
  0.0 8.7 %collective-permute-start = (bf16[1024,512]{1,0:T(8,128)(2,1)}, bf16[1024,512]{1,0:T(8,128)(2,1)S(1)}, u32[]{:S(2)}, u32[]{:S(2)}) collective-permute-start(bf16[1024,512]{1,0:T(8,128)(2,1)} %param.7), channel_id=1, source_target_pairs={{0,1},{1,0},{2,3},{3,2},{4,5},{5,4},{6,7},{7,6},{8,9},{9,8},{10,11... | collective-permute-start | bytes 3145736 | tf_op jit(solution)/shard_map/ppermute | solution.py:95
  8.7 0.9 fusion.2
  9.6 0.9 fusion.1
  10.5 11.3 %all-gather = f16[512,512]{1,0:T(8,128)(2,1)S(1)} all-gather(f16[128,512]{1,0:T(8,128)(2,1)S(1)} %pad_maximum_fusion.2), channel_id=2, replica_groups=mesh['zh'=2,'y'=8,'zl'=4,'x'=4,'core'=2] {'zh','core'}, dimensions={0}, use_global_device_ids=true | all-gather | bytes 655360 | tf_op jit(solution)/shard_map/all_gather | solution.py:78
  22.1 25.0 %all-gather.5 = f16[16,128,512]{2,1,0:T(8,128)(2,1)S(1)} all-gather(f16[2,128,512]{2,1,0:T(8,128)(2,1)S(1)} %pad_maximum_fusion.1), channel_id=1, replica_groups=mesh['zh'=2,'y'=8,'zl'=4,'x'=4,'core'=2] {'y'}, dimensions={0}, use_global_device_ids=true | all-gather | bytes 2359296 | tf_op jit(solution)/shard_map/all_gather | solution.py:90
  47.1 0.2 multiply_convert_fusion.6
  47.4 0.7 fusion.4
  48.1 1.7 %multiply_convert_fusion.5 = f16[512,1024]{1,0:T(8,128)(2,1)} fusion(f32[512,1024]{1,0:T(8,128)S(1)} %fusion.4, bf16[512,512]{1,0:T(8,128)(2,1)S(1)} %bitcast.64, bf16[1024,512]{1,0:T(8,128)(2,1)S(1)} %collective-permute-done), kind=kOutput, calls=%fused_computation.7 | convolution fusion | flops 538443776 | bytes 4718592 | tf_op jit(solution)/shard_map/dot_general | solution.py:99
  49.8 8.6 %all-to-all-start = ((f16[16,32,1024]{2,1,0:T(8,128)(2,1)}), f16[16,32,1024]{2,1,0:T(8,128)(2,1)S(1)}, u32[]{:S(2)}, u32[]{:S(2)}) async-start(f16[16,32,1024]{2,1,0:T(8,128)(2,1)} %bitcast.62), calls=%async_computation | async-start | bytes 2097152 | tf_op jit(solution)/shard_map/all_to_all | solution.py:104
  58.4 0.7 collective-permute-start.1
  59.3 0.2 multiply_convert_fusion.3
  59.6 0.3 copy-done.4
  60.0 0.2 select_reduce_fusion.1
  60.3 0.4 select_reduce_fusion
  60.7 0.1 select_reduce_fusion.2
  60.8 23.2 %all-to-all-done = f16[16,32,1024]{2,1,0:T(8,128)(2,1)S(1)} async-done(((f16[16,32,1024]{2,1,0:T(8,128)(2,1)}), f16[16,32,1024]{2,1,0:T(8,128)(2,1)S(1)}, u32[]{:S(2)}, u32[]{:S(2)}) %all-to-all-start) | async-done | bytes 1048608 | tf_op jit(solution)/shard_map/all_to_all | solution.py:104
  84.0 0.2 convert_reduce_fusion
  84.2 0.7 collective-permute-start.2
  84.9 10.3 %collective-permute-start.3 = (bf16[32,1024]{1,0:T(8,128)(2,1)S(1)}, bf16[32,1024]{1,0:T(8,128)(2,1)S(1)}, u32[]{:S(2)}, u32[]{:S(2)}) collective-permute-start(bf16[32,1024]{1,0:T(8,128)(2,1)S(1)} %get-tuple-element.27), channel_id=1, source_target_pairs={{0,256},{1,257},{2,320},{3,321},{4,384},{5,385},{6,448},{7,449},{8... | collective-permute-start | bytes 196616 | tf_op jit(solution)/shard_map/ppermute | solution.py:113
  95.3 19.9 %all-gather.1 = f16[512,512]{1,0:T(8,128)(2,1)S(1)} all-gather(f16[128,512]{1,0:T(8,128)(2,1)S(1)} %pad_maximum_fusion.3), channel_id=3, replica_groups=mesh['zh'=2,'y'=8,'zl'=4,'x'=4,'core'=2] {'zl'}, dimensions={0}, use_global_device_ids=true | all-gather | bytes 655360 | tf_op jit(solution)/shard_map/all_gather | solution.py:114
  115.2 0.1 slice_bitcast_fusion.1
  115.5 1.1 broadcast_in_dim.68
  116.6 14.1 %all-to-all-start.1 = ((bf16[16,2,32,512]{3,2,1,0:T(8,128)(2,1)}), bf16[16,2,32,512]{3,2,1,0:T(8,128)(2,1)S(1)}, u32[]{:S(2)}, u32[]{:S(2)}) async-start(bf16[16,2,32,512]{3,2,1,0:T(8,128)(2,1)} %bitcast.25), calls=%async_computation.1 | async-start | bytes 2097152 | tf_op jit(solution)/shard_map/all_to_all | solution.py:126
  130.7 0.1 pad_maximum_fusion
  130.9 22.7 %all-gather.6 = f16[4096,512]{1,0:T(8,128)(2,1)S(1)} all-gather(f16[512,512]{1,0:T(8,128)(2,1)S(1)} %pad_maximum_fusion), channel_id=4, replica_groups=mesh['zh'=2,'y'=8,'zl'=4,'x'=4,'core'=2] {'x','core'}, dimensions={0}, use_global_device_ids=true | all-gather | bytes 4718592 | tf_op jit(solution)/shard_map/all_gather | solution.py:127
  153.5 0.5 multiply_convert_fusion.4
  154.0 1.5 multiply_convert_fusion.2
  155.5 1.7 %fusion.6 = f32[512,512]{1,0:T(8,128)} fusion(bf16[1024,512]{1,0:T(8,128)(2,1)S(1)} %bitcast.77, bf16[1024,512]{1,0:T(8,128)(2,1)S(1)} %bitcast.68), kind=kOutput, calls=%fused_computation.46 | convolution fusion | flops 536870912 | bytes 3145728 | tf_op jit(solution)/shard_map/dot_general | solution.py:63
  157.2 1.7 %fusion.5 = f32[512,512]{1,0:T(8,128)} fusion(bf16[1024,512]{1,0:T(8,128)(2,1)S(1)} %bitcast.76, bf16[1024,512]{1,0:T(8,128)(2,1)S(1)} %bitcast.69), kind=kOutput, calls=%fused_computation.45 | convolution fusion | flops 536870912 | bytes 3145728 | tf_op jit(solution)/shard_map/dot_general | solution.py:63
  159.0 2.4 %convolution_add_fusion = f32[512,512]{1,0:T(8,128)S(1)} fusion(f32[512,512]{1,0:T(8,128)} %fusion.6, bf16[1024,512]{1,0:T(8,128)(2,1)} %bitcast.75, bf16[1024,512]{1,0:T(8,128)(2,1)S(1)} %bitcast.70), kind=kOutput, calls=%fused_computation.8 | convolution fusion | flops 537133056 | bytes 4194304 | tf_op jit(solution)/shard_map/dot_general | solution.py:63
  161.3 0.7 convolution_add_fusion.1
  162.1 1.7 %maximum_divide_fusion = f32[1024,512]{1,0:T(8,128)} fusion(f32[512,512]{1,0:T(8,128)S(1)} %convolution_add_fusion, f32[512,512]{1,0:T(8,128)S(1)} %convolution_add_fusion.1, f32[512]{0:T(512)S(1)} %sub.19, f32[1024]{0:T(1024)S(1)} %sub.18), kind=kLoop, calls=%fused_computation | loop fusion | flops 1572864 | bytes 4200448 | tf_op jit(solution)/shard_map/div | solution.py:143
  (39 shorter events, 0.9 us)
Async XLA Ops:
  0.0 48.1 %collective-permute-start = (bf16[1024,512]{1,0:T(8,128)(2,1)}, bf16[1024,512]{1,0:T(8,128)(2,1)S(1)}, u32[]{:S(2)}, u32[]{:S(2)}) collective-permute-start(bf16[1024,512]{1,0:T(8,128)(2,1)} %param.7), channel_id=1, source_target_pairs={{0,1},{1,0},{2,3},{3,2},{4,5},{5,4},{6,7},{7,6},{8,9},{9,8},{10,11... | collective-permute-start | bytes 3145736 | tf_op jit(solution)/shard_map/ppermute | solution.py:95
  22.0 25.3 %copy-start = (bf16[1024,512]{1,0:T(8,128)(2,1)S(1)}, bf16[1024,512]{1,0:T(8,128)(2,1)}, u32[]{:S(2)}) copy-start(bf16[1024,512]{1,0:T(8,128)(2,1)} %param.7) | copy-start | bytes 3145732
  49.8 9.3 %copy-start.2 = (s32[16384]{0:T(1024)S(1)}, s32[16384]{0:T(1024)}, u32[]{:S(2)}) copy-start(s32[16384]{0:T(1024)} %param.11) | copy-start | bytes 196612
  49.8 9.4 %copy-start.1 = (s32[16384]{0:T(1024)S(1)}, s32[16384]{0:T(1024)}, u32[]{:S(2)}) copy-start(s32[16384]{0:T(1024)} %param.10) | copy-start | bytes 196612
  49.8 34.1 %all-to-all-start = ((f16[16,32,1024]{2,1,0:T(8,128)(2,1)}), f16[16,32,1024]{2,1,0:T(8,128)(2,1)S(1)}, u32[]{:S(2)}, u32[]{:S(2)}) async-start(f16[16,32,1024]{2,1,0:T(8,128)(2,1)} %bitcast.62), calls=%async_computation | async-start | bytes 2097152 | tf_op jit(solution)/shard_map/all_to_all | solution.py:104
  58.4 2.4 %collective-permute-start.1 = (f16[64,512]{1,0:T(8,128)(2,1)S(1)}, f16[64,512]{1,0:T(8,128)(2,1)S(1)}, u32[]{:S(2)}, u32[]{:S(2)}) collective-permute-start(f16[64,512]{1,0:T(8,128)(2,1)S(1)} %fusion.2), channel_id=1, source_target_pairs={{0,0},{1,1},{2,32},{3,33},{4,64},{5,65},{6,96},{7,97},{8,128},{9,1... | collective-permute-start | bytes 196616 | tf_op jit(solution)/shard_map/ppermute | solution.py:103
  59.3 0.7 copy-start.4
  59.3 0.8 copy-start.3
  59.3 1.0 dynamic-slice-start.1
  59.3 1.4 dynamic-slice-start
  84.2 31.0 %collective-permute-start.2 = (bf16[32,1024]{1,0:T(8,128)(2,1)S(1)}, bf16[32,1024]{1,0:T(8,128)(2,1)S(1)}, u32[]{:S(2)}, u32[]{:S(2)}) collective-permute-start(bf16[32,1024]{1,0:T(8,128)(2,1)S(1)} %get-tuple-element.27), channel_id=1, source_target_pairs={{0,0},{1,1},{2,64},{3,65},{4,128},{5,129},{6,192},{7,193},{8,256},... | collective-permute-start | bytes 196616 | tf_op jit(solution)/shard_map/ppermute | solution.py:112
  84.9 30.3 %collective-permute-start.3 = (bf16[32,1024]{1,0:T(8,128)(2,1)S(1)}, bf16[32,1024]{1,0:T(8,128)(2,1)S(1)}, u32[]{:S(2)}, u32[]{:S(2)}) collective-permute-start(bf16[32,1024]{1,0:T(8,128)(2,1)S(1)} %get-tuple-element.27), channel_id=1, source_target_pairs={{0,256},{1,257},{2,320},{3,321},{4,384},{5,385},{6,448},{7,449},{8... | collective-permute-start | bytes 196616 | tf_op jit(solution)/shard_map/ppermute | solution.py:113
  116.6 42.3 %all-to-all-start.1 = ((bf16[16,2,32,512]{3,2,1,0:T(8,128)(2,1)}), bf16[16,2,32,512]{3,2,1,0:T(8,128)(2,1)S(1)}, u32[]{:S(2)}, u32[]{:S(2)}) async-start(bf16[16,2,32,512]{3,2,1,0:T(8,128)(2,1)} %bitcast.25), calls=%async_computation.1 | async-start | bytes 2097152 | tf_op jit(solution)/shard_map/all_to_all | solution.py:126
  159.0 2.4 %copy-start.5 = (f32[512,512]{1,0:T(8,128)S(1)}, f32[512,512]{1,0:T(8,128)}, u32[]{:S(2)}) copy-start(f32[512,512]{1,0:T(8,128)} %fusion.5) | copy-start | bytes 3145732
where the time goes:
time: 164 us
  blocking collectives  78.9 us (48%)
  starting transfers between devices  43 us (26%)
  waiting for transfers between devices  23.2 us (14%)
  matrix products  8.97 us (5%)
  other arithmetic  7.21 us (4%)
  local copies, waits for them, and re-layouts  2.06 us (1%)
    all_gather x1, blocking collectives, per_device(): factors = lax.all_gather(chunk, 'y', axis=0, tiled=True)  25 us
    all_to_all x1, waiting for transfers between devices, per_device(): arrived = lax.all_to_all(sent, AUX_COL, 0, 0)  23.2 us
    all_gather x1, blocking collectives, per_device(): both = lax.all_gather(both, ('x', 'core'), axis=0).reshape(4, 2, 512, cols)  22.7 us
    all_gather x1, blocking collectives, per_device(): lax.all_gather(jnp.concatenate([right_moved, light], axis=0), 'zl', axis=0)  19.9 us
    all_to_all x1, starting transfers between devices, per_device(): lax.all_to_all(mirror.reshape(16, 2, 32, cols), ('y', 'core'), 0, 0)  14.1 us
    all_gather x1, blocking collectives, per_device(): lax.all_gather(jnp.concatenate([left, right], axis=0), ('zh', 'core'), ax...  11.3 us
    ppermute x1, starting transfers between devices, per_device(): cross = lax.ppermute(fitted, ALL, chips(to_column, 1))  10.3 us
    ppermute x1, starting transfers between devices, per_device(): other_amplitudes = lax.ppermute(amplitudes, 'core', SWAP)  8.74 us
  transfers between devices with their start and end apart: 6, of which 1 were waited for; matrix products, arithmetic and copies ran while one was open for 6% of the time, Pallas kernels for 0%

commit v1 on v0

--- a/solution.py
+++ b/solution.py
@@ -73,19 +73,19 @@
     row_block = lax.axis_index(ROW)
     col_block = lax.axis_index(COL + ("core",))
 
-    left = pack(aux_left.T, LEFT_SCALE)
-    right = pack(aux_right.T, RIGHT_SCALE)
-    near = lax.all_gather(jnp.concatenate([left, right], axis=0), ("zh", "core"), axis=0)
-    near = near.reshape(2, 2, 2 * left.shape[0], cols)
+    pair = jnp.concatenate([aux_left.T, aux_right.T], axis=0)
+    near = lax.all_gather(pair, ("zh", "core"), axis=0).reshape(2, 2, 128, cols)
     mine = lax.dynamic_index_in_dim(near, core, 1, keepdims=False)
     theirs = lax.dynamic_index_in_dim(near, 1 - core, 1, keepdims=False)
-    chunk = jnp.concatenate(
+    left_near = jnp.concatenate(
         [
             lax.dynamic_slice_in_dim(mine, core * 32, 32, 1),
             lax.dynamic_slice_in_dim(theirs, core * 32, 32, 1),
-            mine[:, 64:],
         ],
         axis=1,
+    )
+    chunk = jnp.concatenate(
+        [pack(left_near, LEFT_SCALE), pack(mine[:, 64:], RIGHT_SCALE)], axis=1
     )
     factors = lax.all_gather(chunk, "y", axis=0, tiled=True)
     left_kept = restore(factors[:, :32], LEFT_SCALE).reshape(512, cols)
@@ -100,7 +100,7 @@
         left_taken, other_amplitudes, (((1,), (1,)), ((), ())), preferred_element_type=jnp.float32
     )
     sent = (partial * SUM_SCALE).astype(jnp.float16).reshape(16, 32, rows)
-    right_moved = lax.ppermute(right, ALL, chips(to_row))
+    right_moved = lax.ppermute(pack(aux_right.T, RIGHT_SCALE), ALL, chips(to_row))
     arrived = lax.all_to_all(sent, AUX_COL, 0, 0)
     arrived, right_moved = lax.optimization_barrier((arrived, right_moved))
     summed = jnp.sum(arrived.astype(jnp.float32), axis=0) * (1.0 / SUM_SCALE)
@@ -111,12 +111,6 @@
 
     same = lax.ppermute(fitted, ALL, chips(to_column))
     cross = lax.ppermute(fitted, ALL, chips(to_column, 1))
-    both = lax.all_gather(jnp.concatenate([right_moved, light], axis=0), "zl", axis=0)
-    both, same, cross = lax.optimization_barrier((both, same, cross))
-    both = both.reshape(2, 2, 4, 32, cols)
-    right_part = both[:, :, :2].transpose(0, 2, 1, 3, 4).reshape(256, cols)
-    fitted_part = both[:, :, 2:].transpose(2, 0, 1, 3, 4).reshape(256, cols)
-    both = jnp.concatenate([right_part, fitted_part], axis=0)
     low = lax.axis_index("zh") == 0
     below, above = jnp.where(low, same, cross), jnp.where(low, cross, same)
     mirror_chunk = jnp.stack(
@@ -124,6 +118,11 @@
     )
     mirror = jnp.broadcast_to(mirror_chunk[None], (8,) + mirror_chunk.shape)
     mirror = lax.all_to_all(mirror.reshape(16, 2, 32, cols), ("y", "core"), 0, 0)
+    both = lax.all_gather(jnp.concatenate([right_moved, light], axis=0), "zl", axis=0)
+    both = both.reshape(2, 2, 4, 32, cols)
+    right_part = both[:, :, :2].transpose(0, 2, 1, 3, 4).reshape(256, cols)
+    fitted_part = both[:, :, 2:].transpose(2, 0, 1, 3, 4).reshape(256, cols)
+    both = jnp.concatenate([right_part, fitted_part], axis=0)
     both = lax.all_gather(both, ("x", "core"), axis=0).reshape(4, 2, 512, cols)
     mirror = mirror.reshape(1024, cols)
 

time: 164 us -> 163 us (level)
  no operation moved by 1% of the time
where the time goes in v1:
time: 163 us
  blocking collectives  80.5 us (49%)
  starting transfers between devices  41.5 us (25%)
  waiting for transfers between devices  23.2 us (14%)
  matrix products  8.71 us (5%)
  other arithmetic  6.42 us (4%)
  local copies, waits for them, and re-layouts  2 us (1%)
    all_gather x1, blocking collectives, per_device(): factors = lax.all_gather(chunk, 'y', axis=0, tiled=True)  25 us
    all_gather x1, blocking collectives, per_device(): both = lax.all_gather(both, ('x', 'core'), axis=0).reshape(4, 2, 512, cols)  23.7 us
    all_to_all x1, waiting for transfers between devices, per_device(): arrived = lax.all_to_all(sent, AUX_COL, 0, 0)  23.1 us
    all_gather x1, blocking collectives, per_device(): lax.all_gather(jnp.concatenate([right_moved, light], axis=0), 'zl', axis=0)  20.5 us
    all_to_all x1, starting transfers between devices, per_device(): lax.all_to_all(mirror.reshape(16, 2, 32, cols), ('y', 'core'), 0, 0)  12.5 us
    all_gather x1, blocking collectives, per_device(): near = lax.all_gather(pair, ('zh', 'core'), axis=0).reshape(2, 2, 128, cols)  11.3 us
    ppermute x1, starting transfers between devices, per_device(): cross = lax.ppermute(fitted, ALL, chips(to_column, 1))  10.3 us
    ppermute x1, starting transfers between devices, per_device(): other_amplitudes = lax.ppermute(amplitudes, 'core', SWAP)  8.74 us
  transfers between devices with their start and end apart: 6, of which 1 were waited for; matrix products, arithmetic and copies ran while one was open for 6% of the time, Pallas kernels for 0%

profile of v1, /device:TPU:1, one launch (start us, length us, event | category | flops | bytes accessed | tf_op | source)
XLA Modules:
  0.0 162.6 jit_solution(9226933866115589744)
XLA Ops:
  0.0 8.7 %collective-permute-start = (bf16[1024,512]{1,0:T(8,128)(2,1)}, bf16[1024,512]{1,0:T(8,128)(2,1)S(1)}, u32[]{:S(2)}, u32[]{:S(2)}) collective-permute-start(bf16[1024,512]{1,0:T(8,128)(2,1)} %param.7), channel_id=1, source_target_pairs={{0,1},{1,0},{2,3},{3,2},{4,5},{5,4},{6,7},{7,6},{8,9},{9,8},{10,11... | collective-permute-start | bytes 3145736 | tf_op jit(solution)/shard_map/ppermute | solution.py:95
  8.7 0.9 pad_maximum_fusion.2
  9.6 11.3 %all-gather = bf16[512,512]{1,0:T(8,128)(2,1)S(1)} all-gather(bf16[128,512]{1,0:T(8,128)(2,1)S(1)} %pad_maximum_fusion.2), channel_id=2, replica_groups=mesh['zh'=2,'y'=8,'zl'=4,'x'=4,'core'=2] {'zh','core'}, dimensions={0}, use_global_device_ids=true | all-gather | bytes 655360 | tf_op jit(solution)/shard_map/all_gather | solution.py:77
  21.2 25.0 %all-gather.5 = f16[16,128,512]{2,1,0:T(8,128)(2,1)S(1)} all-gather(f16[2,128,512]{2,1,0:T(8,128)(2,1)S(1)} %pad_maximum_fusion.1), channel_id=1, replica_groups=mesh['zh'=2,'y'=8,'zl'=4,'x'=4,'core'=2] {'y'}, dimensions={0}, use_global_device_ids=true | all-gather | bytes 2359296 | tf_op jit(solution)/shard_map/all_gather | solution.py:90
  46.2 0.2 multiply_convert_fusion.6
  46.5 0.7 fusion.2
  47.2 1.7 %multiply_convert_fusion.5 = f16[512,1024]{1,0:T(8,128)(2,1)} fusion(f32[512,1024]{1,0:T(8,128)S(1)} %fusion.2, bf16[512,512]{1,0:T(8,128)(2,1)S(1)} %bitcast.56, bf16[1024,512]{1,0:T(8,128)(2,1)S(1)} %collective-permute-done), kind=kOutput, calls=%fused_computation.7 | convolution fusion | flops 538443776 | bytes 4718592 | tf_op jit(solution)/shard_map/dot_general | solution.py:99
  49.0 8.6 %all-to-all-start = ((f16[16,32,1024]{2,1,0:T(8,128)(2,1)}), f16[16,32,1024]{2,1,0:T(8,128)(2,1)S(1)}, u32[]{:S(2)}, u32[]{:S(2)}) async-start(f16[16,32,1024]{2,1,0:T(8,128)(2,1)} %bitcast.54), calls=%async_computation | async-start | bytes 2097152 | tf_op jit(solution)/shard_map/all_to_all | solution.py:104
  57.6 0.7 collective-permute-start.1
  58.4 0.2 multiply_convert_fusion.3
  58.7 0.1 copy.17
  58.8 0.3 copy-done.6
  59.2 0.2 select_reduce_fusion.1
  59.4 0.4 select_reduce_fusion
  59.8 0.1 select_reduce_fusion.2
  59.9 23.1 %all-to-all-done = f16[16,32,1024]{2,1,0:T(8,128)(2,1)S(1)} async-done(((f16[16,32,1024]{2,1,0:T(8,128)(2,1)}), f16[16,32,1024]{2,1,0:T(8,128)(2,1)S(1)}, u32[]{:S(2)}, u32[]{:S(2)}) %all-to-all-start) | async-done | bytes 1048608 | tf_op jit(solution)/shard_map/all_to_all | solution.py:104
  83.1 0.2 convert_reduce_fusion
  83.3 0.7 collective-permute-start.2
  84.0 10.3 %collective-permute-start.3 = (bf16[32,1024]{1,0:T(8,128)(2,1)S(1)}, bf16[32,1024]{1,0:T(8,128)(2,1)S(1)}, u32[]{:S(2)}, u32[]{:S(2)}) collective-permute-start(bf16[32,1024]{1,0:T(8,128)(2,1)S(1)} %get-tuple-element.21), channel_id=1, source_target_pairs={{0,256},{1,257},{2,320},{3,321},{4,384},{5,385},{6,448},{7,449},{8... | collective-permute-start | bytes 196616 | tf_op jit(solution)/shard_map/ppermute | solution.py:113
  94.4 20.5 %all-gather.1 = f16[512,512]{1,0:T(8,128)(2,1)S(1)} all-gather(f16[128,512]{1,0:T(8,128)(2,1)S(1)} %pad_maximum_fusion.3), channel_id=3, replica_groups=mesh['zh'=2,'y'=8,'zl'=4,'x'=4,'core'=2] {'zl'}, dimensions={0}, use_global_device_ids=true | all-gather | bytes 655360 | tf_op jit(solution)/shard_map/all_gather | solution.py:121
  114.9 0.1 slice_bitcast_fusion.1
  115.1 0.1 pad_maximum_fusion
  115.4 1.1 broadcast_in_dim.68
  116.5 12.5 %all-to-all-start.1 = ((bf16[16,2,32,512]{3,2,1,0:T(8,128)(2,1)}), bf16[16,2,32,512]{3,2,1,0:T(8,128)(2,1)S(1)}, u32[]{:S(2)}, u32[]{:S(2)}) async-start(bf16[16,2,32,512]{3,2,1,0:T(8,128)(2,1)} %bitcast.24), calls=%async_computation.1 | async-start | bytes 2097152 | tf_op jit(solution)/shard_map/all_to_all | solution.py:120
  129.0 23.7 %all-gather.6 = f16[4096,512]{1,0:T(8,128)(2,1)S(1)} all-gather(f16[512,512]{1,0:T(8,128)(2,1)S(1)} %pad_maximum_fusion), channel_id=4, replica_groups=mesh['zh'=2,'y'=8,'zl'=4,'x'=4,'core'=2] {'x','core'}, dimensions={0}, use_global_device_ids=true | all-gather | bytes 4718592 | tf_op jit(solution)/shard_map/all_gather | solution.py:126
  152.6 0.5 multiply_convert_fusion.4
  153.2 1.5 multiply_convert_fusion.2
  154.7 1.7 %fusion.4 = f32[512,512]{1,0:T(8,128)} fusion(bf16[1024,512]{1,0:T(8,128)(2,1)S(1)} %bitcast.69, bf16[1024,512]{1,0:T(8,128)(2,1)S(1)} %bitcast.60), kind=kOutput, calls=%fused_computation.45 | convolution fusion | flops 536870912 | bytes 3145728 | tf_op jit(solution)/shard_map/dot_general | solution.py:63
  156.4 1.7 %fusion.3 = f32[512,512]{1,0:T(8,128)} fusion(bf16[1024,512]{1,0:T(8,128)(2,1)S(1)} %bitcast.68, bf16[1024,512]{1,0:T(8,128)(2,1)S(1)} %bitcast.61), kind=kOutput, calls=%fused_computation.44 | convolution fusion | flops 536870912 | bytes 3145728 | tf_op jit(solution)/shard_map/dot_general | solution.py:63
  158.1 2.1 %convolution_add_fusion = f32[512,512]{1,0:T(8,128)S(1)} fusion(f32[512,512]{1,0:T(8,128)} %fusion.4, bf16[1024,512]{1,0:T(8,128)(2,1)S(1)} %bitcast.67, bf16[1024,512]{1,0:T(8,128)(2,1)S(1)} %bitcast.62), kind=kOutput, calls=%fused_computation.8 | convolution fusion | flops 537133056 | bytes 4194304 | tf_op jit(solution)/shard_map/dot_general | solution.py:63
  160.2 0.7 convolution_add_fusion.1
  160.9 1.7 %maximum_divide_fusion = f32[1024,512]{1,0:T(8,128)} fusion(f32[512,512]{1,0:T(8,128)S(1)} %convolution_add_fusion, f32[512,512]{1,0:T(8,128)S(1)} %convolution_add_fusion.1, f32[512]{0:T(512)S(1)} %sub.19, f32[1024]{0:T(1024)S(1)} %sub.18), kind=kLoop, calls=%fused_computation | loop fusion | flops 1572864 | bytes 4200448 | tf_op jit(solution)/shard_map/div | solution.py:142
  (43 shorter events, 0.8 us)
Async XLA Ops:
  0.0 47.2 %collective-permute-start = (bf16[1024,512]{1,0:T(8,128)(2,1)}, bf16[1024,512]{1,0:T(8,128)(2,1)S(1)}, u32[]{:S(2)}, u32[]{:S(2)}) collective-permute-start(bf16[1024,512]{1,0:T(8,128)(2,1)} %param.7), channel_id=1, source_target_pairs={{0,1},{1,0},{2,3},{3,2},{4,5},{5,4},{6,7},{7,6},{8,9},{9,8},{10,11... | collective-permute-start | bytes 3145736 | tf_op jit(solution)/shard_map/ppermute | solution.py:95
  21.2 25.3 %copy-start = (bf16[1024,512]{1,0:T(8,128)(2,1)S(1)}, bf16[1024,512]{1,0:T(8,128)(2,1)}, u32[]{:S(2)}) copy-start(bf16[1024,512]{1,0:T(8,128)(2,1)} %param.7) | copy-start | bytes 3145732
  49.0 8.6 %copy-start.2 = (bf16[512,64]{0,1:T(8,128)(2,1)S(1)}, bf16[512,64]{0,1:T(8,128)(2,1)}, u32[]{:S(2)}) copy-start(bf16[512,64]{0,1:T(8,128)(2,1)} %param.9) | copy-start | bytes 196612
  49.0 9.3 %copy-start.4 = (s32[16384]{0:T(1024)S(1)}, s32[16384]{0:T(1024)}, u32[]{:S(2)}) copy-start(s32[16384]{0:T(1024)} %param.11) | copy-start | bytes 196612
  49.0 9.4 %copy-start.3 = (s32[16384]{0:T(1024)S(1)}, s32[16384]{0:T(1024)}, u32[]{:S(2)}) copy-start(s32[16384]{0:T(1024)} %param.10) | copy-start | bytes 196612
  49.0 34.1 %all-to-all-start = ((f16[16,32,1024]{2,1,0:T(8,128)(2,1)}), f16[16,32,1024]{2,1,0:T(8,128)(2,1)S(1)}, u32[]{:S(2)}, u32[]{:S(2)}) async-start(f16[16,32,1024]{2,1,0:T(8,128)(2,1)} %bitcast.54), calls=%async_computation | async-start | bytes 2097152 | tf_op jit(solution)/shard_map/all_to_all | solution.py:104
  57.6 2.4 %collective-permute-start.1 = (f16[64,512]{1,0:T(8,128)(2,1)S(1)}, f16[64,512]{1,0:T(8,128)(2,1)S(1)}, u32[]{:S(2)}, u32[]{:S(2)}) collective-permute-start(f16[64,512]{1,0:T(8,128)(2,1)S(1)} %multiply_convert_fusion.11), channel_id=1, source_target_pairs={{0,0},{1,1},{2,32},{3,33},{4,64},{5,65},{6,96},{7,97},{8,128},{9,1... | collective-permute-start | bytes 196616 | tf_op jit(solution)/shard_map/ppermute | solution.py:103
  58.4 0.7 copy-start.6
  58.4 0.8 copy-start.5
  58.4 1.0 dynamic-slice-start.1
  58.4 1.4 dynamic-slice-start
  83.3 31.9 %collective-permute-start.2 = (bf16[32,1024]{1,0:T(8,128)(2,1)S(1)}, bf16[32,1024]{1,0:T(8,128)(2,1)S(1)}, u32[]{:S(2)}, u32[]{:S(2)}) collective-permute-start(bf16[32,1024]{1,0:T(8,128)(2,1)S(1)} %get-tuple-element.21), channel_id=1, source_target_pairs={{0,0},{1,1},{2,64},{3,65},{4,128},{5,129},{6,192},{7,193},{8,256},... | collective-permute-start | bytes 196616 | tf_op jit(solution)/shard_map/ppermute | solution.py:112
  84.0 31.3 %collective-permute-start.3 = (bf16[32,1024]{1,0:T(8,128)(2,1)S(1)}, bf16[32,1024]{1,0:T(8,128)(2,1)S(1)}, u32[]{:S(2)}, u32[]{:S(2)}) collective-permute-start(bf16[32,1024]{1,0:T(8,128)(2,1)S(1)} %get-tuple-element.21), channel_id=1, source_target_pairs={{0,256},{1,257},{2,320},{3,321},{4,384},{5,385},{6,448},{7,449},{8... | collective-permute-start | bytes 196616 | tf_op jit(solution)/shard_map/ppermute | solution.py:113
  116.5 41.6 %all-to-all-start.1 = ((bf16[16,2,32,512]{3,2,1,0:T(8,128)(2,1)}), bf16[16,2,32,512]{3,2,1,0:T(8,128)(2,1)S(1)}, u32[]{:S(2)}, u32[]{:S(2)}) async-start(bf16[16,2,32,512]{3,2,1,0:T(8,128)(2,1)} %bitcast.24), calls=%async_computation.1 | async-start | bytes 2097152 | tf_op jit(solution)/shard_map/all_to_all | solution.py:120
  158.1 2.1 %copy-start.1 = (bf16[4,1,256,512]{3,2,1,0:T(8,128)(2,1)S(1)}, bf16[4,1,256,512]{3,2,1,0:T(8,128)(2,1)}, u32[]{:S(2)}) copy-start(bf16[4,1,256,512]{3,2,1,0:T(8,128)(2,1)} %get-tuple-element.9) | copy-start | bytes 3145732
  158.1 2.1 %copy-start.7 = (f32[512,512]{1,0:T(8,128)S(1)}, f32[512,512]{1,0:T(8,128)}, u32[]{:S(2)}) copy-start(f32[512,512]{1,0:T(8,128)} %fusion.3) | copy-start | bytes 3145732

commit v2 on v1

--- a/solution.py
+++ b/solution.py
@@ -8,7 +8,6 @@
 
 ROW = ("zh", "y")
 COL = ("zl", "x")
-AUX_COL = ("x", "zl")
 ALL = ("zh", "y", "zl", "x", "core")
 SIZES = (2, 8, 4, 4, 2)
 SWAP = [(0, 1), (1, 0)]
@@ -16,6 +15,7 @@
 RIGHT_SCALE = 2.0**18
 FIT_SCALE = 8.0
 SUM_SCALE = 128.0
+LINE_SCALE = 32.0
 
 
 def device_of(zh, y, zl, x, core):
@@ -31,8 +31,8 @@
 
 
 def to_column(zh, y, zl, x):
-    slot, block = x * 4 + zl, zh * 8 + y
-    return slot & 1, slot >> 1, block // 4, block % 4
+    block = zh * 8 + y
+    return x >> 1, zl * 2 + (x & 1), block // 4, block % 4
 
 
 def to_row(zh, y, zl, x):
@@ -88,10 +88,12 @@
         [pack(left_near, LEFT_SCALE), pack(mine[:, 64:], RIGHT_SCALE)], axis=1
     )
     factors = lax.all_gather(chunk, "y", axis=0, tiled=True)
-    left_kept = restore(factors[:, :32], LEFT_SCALE).reshape(512, cols)
-    left_taken = restore(factors[:, 32:64], LEFT_SCALE).reshape(512, cols)
-    right_cols = restore(factors[:, 64:], RIGHT_SCALE).reshape(4, 4, 2, 32, cols)
-    right_cols = right_cols.transpose(0, 2, 1, 3, 4).reshape(1024, cols)
+    factors = factors.reshape(2, 2, 2, 2, 128, cols)
+    by_slot = factors.transpose(3, 2, 0, 1, 4, 5)
+    left_kept = restore(by_slot[..., :32, :], LEFT_SCALE).reshape(512, cols)
+    left_taken = restore(by_slot[..., 32:64, :], LEFT_SCALE).reshape(512, cols)
+    right_cols = by_slot[..., 64:, :].reshape(4, 4, 2, 32, cols).transpose(0, 2, 1, 3, 4)
+    right_cols = restore(right_cols, RIGHT_SCALE).reshape(1024, cols)
     other_amplitudes = lax.ppermute(amplitudes, "core", SWAP)
 
     partial = lax.dot_general(
@@ -99,11 +101,14 @@
     ) + lax.dot_general(
         left_taken, other_amplitudes, (((1,), (1,)), ((), ())), preferred_element_type=jnp.float32
     )
-    sent = (partial * SUM_SCALE).astype(jnp.float16).reshape(16, 32, rows)
+    sent = (partial * SUM_SCALE).astype(jnp.float16).reshape(4, 128, rows)
     right_moved = lax.ppermute(pack(aux_right.T, RIGHT_SCALE), ALL, chips(to_row))
-    arrived = lax.all_to_all(sent, AUX_COL, 0, 0)
+    arrived = lax.all_to_all(sent, "x", 0, 0)
+    summed = jnp.sum(arrived.astype(jnp.float32), axis=0) * (LINE_SCALE / SUM_SCALE)
+    sent = summed.astype(jnp.float16).reshape(4, 32, rows)
+    arrived = lax.all_to_all(sent, "zl", 0, 0)
     arrived, right_moved = lax.optimization_barrier((arrived, right_moved))
-    summed = jnp.sum(arrived.astype(jnp.float32), axis=0) * (1.0 / SUM_SCALE)
+    summed = jnp.sum(arrived.astype(jnp.float32), axis=0) * (1.0 / LINE_SCALE)
     rounded = lax.reduce_precision(summed, exponent_bits=8, mantissa_bits=7)
     fitted = rounded.astype(jnp.bfloat16)
     light = (rounded * FIT_SCALE).astype(jnp.float16)
@@ -111,6 +116,12 @@
 
     same = lax.ppermute(fitted, ALL, chips(to_column))
     cross = lax.ppermute(fitted, ALL, chips(to_column, 1))
+    both = lax.all_gather(jnp.concatenate([right_moved, light], axis=0), "zl", axis=0)
+    both, same, cross = lax.optimization_barrier((both, same, cross))
+    both = both.reshape(2, 2, 4, 32, cols)
+    right_part = both[:, :, :2].transpose(0, 2, 1, 3, 4).reshape(256, cols)
+    fitted_part = both[:, :, 2:].transpose(2, 0, 1, 3, 4).reshape(256, cols)
+    both = jnp.concatenate([right_part, fitted_part], axis=0)
     low = lax.axis_index("zh") == 0
     below, above = jnp.where(low, same, cross), jnp.where(low, cross, same)
     mirror_chunk = jnp.stack(
@@ -118,11 +129,6 @@
     )
     mirror = jnp.broadcast_to(mirror_chunk[None], (8,) + mirror_chunk.shape)
     mirror = lax.all_to_all(mirror.reshape(16, 2, 32, cols), ("y", "core"), 0, 0)
-    both = lax.all_gather(jnp.concatenate([right_moved, light], axis=0), "zl", axis=0)
-    both = both.reshape(2, 2, 4, 32, cols)
-    right_part = both[:, :, :2].transpose(0, 2, 1, 3, 4).reshape(256, cols)
-    fitted_part = both[:, :, 2:].transpose(2, 0, 1, 3, 4).reshape(256, cols)
-    both = jnp.concatenate([right_part, fitted_part], axis=0)
     both = lax.all_gather(both, ("x", "core"), axis=0).reshape(4, 2, 512, cols)
     mirror = mirror.reshape(1024, cols)
 

time: 163 us -> 158 us (0.969)
  the two profiles are of different devices: /device:TPU:1 before, /device:TPU:2 now
where the time goes in v2:
time: 158 us; the launch traced here: 156 us
  blocking collectives  83.8 us (53%)
  starting transfers between devices  38.6 us (24%)
  waiting for transfers between devices  12.1 us (8%)
  matrix products  8.97 us (6%)
  other arithmetic  8.57 us (5%)
  local copies, waits for them, and re-layouts  3.17 us (2%)
    all_gather x1, blocking collectives, per_device(): factors = lax.all_gather(chunk, 'y', axis=0, tiled=True)  31.6 us
    all_gather x1, blocking collectives, per_device(): both = lax.all_gather(both, ('x', 'core'), axis=0).reshape(4, 2, 512, cols)  21.5 us
    all_gather x1, blocking collectives, per_device(): lax.all_gather(jnp.concatenate([right_moved, light], axis=0), 'zl', axis=0)  15.8 us
    all_gather x1, blocking collectives, per_device(): near = lax.all_gather(pair, ('zh', 'core'), axis=0).reshape(2, 2, 128, cols)  14.8 us
    all_to_all x1, starting transfers between devices, per_device(): lax.all_to_all(mirror.reshape(16, 2, 32, cols), ('y', 'core'), 0, 0)  12.5 us
    all_to_all x1, waiting for transfers between devices, per_device(): arrived = lax.all_to_all(sent, 'x', 0, 0)  6.96 us
    ppermute x1, starting transfers between devices, per_device(): cross = lax.ppermute(fitted, ALL, chips(to_column, 1))  6.76 us
    dot_general x4, matrix products, contract(): lax.dot_general(left, right, (((0,), (0,)), ((), ())), preferred_element_...  6.49 us
  transfers between devices with their start and end apart: 7, of which 2 were waited for; matrix products, arithmetic and copies ran while one was open for 7% of the time, Pallas kernels for 0%

profile of v2, /device:TPU:2, one launch (start us, length us, event | category | flops | bytes accessed | tf_op | source)
XLA Modules:
  0.0 155.6 jit_solution(5702923340349716)
XLA Ops:
  0.0 1.9 %collective-permute-start = (bf16[1024,512]{1,0:T(8,128)(2,1)}, bf16[1024,512]{1,0:T(8,128)(2,1)S(1)}, u32[]{:S(2)}, u32[]{:S(2)}) collective-permute-start(bf16[1024,512]{1,0:T(8,128)(2,1)} %param.7), channel_id=1, source_target_pairs={{0,1},{1,0},{2,3},{3,2},{4,5},{5,4},{6,7},{7,6},{8,9},{9,8},{10,11... | collective-permute-start | bytes 3145736 | tf_op jit(solution)/shard_map/ppermute | solution.py:97
  1.9 0.9 pad_maximum_fusion.2
  2.8 14.8 %all-gather = bf16[512,512]{1,0:T(8,128)(2,1)S(1)} all-gather(bf16[128,512]{1,0:T(8,128)(2,1)S(1)} %pad_maximum_fusion.2), channel_id=2, replica_groups=mesh['zh'=2,'y'=8,'zl'=4,'x'=4,'core'=2] {'zh','core'}, dimensions={0}, use_global_device_ids=true | all-gather | bytes 655360 | tf_op jit(solution)/shard_map/all_gather | solution.py:77
  17.9 31.6 %all-gather.5 = f16[16,128,512]{2,1,0:T(8,128)(2,1)S(1)} all-gather(f16[2,128,512]{2,1,0:T(8,128)(2,1)S(1)} %pad_maximum_fusion.1), channel_id=1, replica_groups=mesh['zh'=2,'y'=8,'zl'=4,'x'=4,'core'=2] {'y'}, dimensions={0}, use_global_device_ids=true | all-gather | bytes 2359296 | tf_op jit(solution)/shard_map/all_gather | solution.py:90
  49.5 0.3 multiply_convert_fusion.6
  49.9 0.8 copy-done
  50.7 0.7 fusion.2
  51.5 1.7 %multiply_convert_fusion.5 = f16[512,1024]{1,0:T(8,128)(2,1)} fusion(f32[512,1024]{1,0:T(8,128)S(1)} %fusion.2, bf16[512,512]{1,0:T(8,128)(2,1)S(1)} %bitcast.67, bf16[1024,512]{1,0:T(8,128)(2,1)S(1)} %collective-permute-done), kind=kOutput, calls=%fused_computation.7 | convolution fusion | flops 538443776 | bytes 4718592 | tf_op jit(solution)/shard_map/dot_general | solution.py:101
  53.2 5.1 %all-to-all-start = ((f16[4,128,1024]{2,1,0:T(8,128)(2,1)}), f16[4,128,1024]{2,1,0:T(8,128)(2,1)}, u32[]{:S(2)}, u32[]{:S(2)}) async-start(f16[4,128,1024]{2,1,0:T(8,128)(2,1)} %bitcast.11), calls=%async_computation | async-start | bytes 2097152 | tf_op jit(solution)/shard_map/all_to_all | solution.py:106
  58.4 2.2 %collective-permute-start.1 = (f16[64,512]{1,0:T(8,128)(2,1)S(1)}, f16[64,512]{1,0:T(8,128)(2,1)S(1)}, u32[]{:S(2)}, u32[]{:S(2)}) collective-permute-start(f16[64,512]{1,0:T(8,128)(2,1)S(1)} %multiply_convert_fusion.12), channel_id=1, source_target_pairs={{0,0},{1,1},{2,32},{3,33},{4,64},{5,65},{6,96},{7,97},{8,128},{9,1... | collective-permute-start | bytes 196616 | tf_op jit(solution)/shard_map/ppermute | solution.py:105
  60.7 0.2 multiply_convert_fusion.3
  60.9 7.0 %all-to-all-done = f16[4,128,1024]{2,1,0:T(8,128)(2,1)} async-done(((f16[4,128,1024]{2,1,0:T(8,128)(2,1)}), f16[4,128,1024]{2,1,0:T(8,128)(2,1)}, u32[]{:S(2)}, u32[]{:S(2)}) %all-to-all-start) | async-done | bytes 1048608 | tf_op jit(solution)/shard_map/all_to_all | solution.py:106
  67.9 1.5 convert_reduce_fusion
  69.4 0.8 multiply_convert_fusion.8
  70.1 6.3 %all-to-all-start.1 = ((f16[4,32,1024]{2,1,0:T(8,128)(2,1)}), f16[4,32,1024]{2,1,0:T(8,128)(2,1)S(1)}, u32[]{:S(2)}, u32[]{:S(2)}) async-start(f16[4,32,1024]{2,1,0:T(8,128)(2,1)} %bitcast.12), calls=%async_computation.1 | async-start | bytes 524288 | tf_op jit(solution)/shard_map/all_to_all | solution.py:109
  76.8 0.5 copy-done.4
  77.3 0.2 select_reduce_fusion.1
  77.6 0.4 select_reduce_fusion
  78.1 5.1 %all-to-all-done.1 = f16[4,32,1024]{2,1,0:T(8,128)(2,1)S(1)} async-done(((f16[4,32,1024]{2,1,0:T(8,128)(2,1)}), f16[4,32,1024]{2,1,0:T(8,128)(2,1)S(1)}, u32[]{:S(2)}, u32[]{:S(2)}) %all-to-all-start.1) | async-done | bytes 262176 | tf_op jit(solution)/shard_map/all_to_all | solution.py:109
  83.3 3.8 %collective-permute-start.2 = (bf16[32,1024]{1,0:T(8,128)(2,1)S(1)}, bf16[32,1024]{1,0:T(8,128)(2,1)S(1)}, u32[]{:S(2)}, u32[]{:S(2)}) collective-permute-start(bf16[32,1024]{1,0:T(8,128)(2,1)S(1)} %get-tuple-element.27), channel_id=1, source_target_pairs={{0,0},{1,1},{2,32},{3,33},{4,256},{5,257},{6,288},{7,289},{8,64},{... | collective-permute-start | bytes 196616 | tf_op jit(solution)/shard_map/ppermute | solution.py:117
  87.1 6.8 %collective-permute-start.3 = (bf16[32,1024]{1,0:T(8,128)(2,1)S(1)}, bf16[32,1024]{1,0:T(8,128)(2,1)S(1)}, u32[]{:S(2)}, u32[]{:S(2)}) collective-permute-start(bf16[32,1024]{1,0:T(8,128)(2,1)S(1)} %get-tuple-element.27), channel_id=1, source_target_pairs={{0,256},{1,257},{2,288},{3,289},{4,0},{5,1},{6,32},{7,33},{8,320},... | collective-permute-start | bytes 196616 | tf_op jit(solution)/shard_map/ppermute | solution.py:118
  94.0 15.8 %all-gather.1 = f16[512,512]{1,0:T(8,128)(2,1)S(1)} all-gather(f16[128,512]{1,0:T(8,128)(2,1)S(1)} %pad_maximum_fusion.3), channel_id=3, replica_groups=mesh['zh'=2,'y'=8,'zl'=4,'x'=4,'core'=2] {'zl'}, dimensions={0}, use_global_device_ids=true | all-gather | bytes 655360 | tf_op jit(solution)/shard_map/all_gather | solution.py:119
  110.1 1.1 broadcast_in_dim.68
  111.2 12.5 %all-to-all-start.2 = ((bf16[16,2,32,512]{3,2,1,0:T(8,128)(2,1)}), bf16[16,2,32,512]{3,2,1,0:T(8,128)(2,1)S(1)}, u32[]{:S(2)}, u32[]{:S(2)}) async-start(bf16[16,2,32,512]{3,2,1,0:T(8,128)(2,1)} %bitcast.29), calls=%async_computation.2 | async-start | bytes 2097152 | tf_op jit(solution)/shard_map/all_to_all | solution.py:131
  123.8 21.5 %all-gather.6 = f16[4096,512]{1,0:T(8,128)(2,1)S(1)} all-gather(f16[512,512]{1,0:T(8,128)(2,1)S(1)} %pad_maximum_fusion), channel_id=4, replica_groups=mesh['zh'=2,'y'=8,'zl'=4,'x'=4,'core'=2] {'x','core'}, dimensions={0}, use_global_device_ids=true | all-gather | bytes 4718592 | tf_op jit(solution)/shard_map/all_gather | solution.py:132
  145.3 0.5 multiply_convert_fusion.4
  145.9 1.5 multiply_convert_fusion.2
  147.4 1.7 %fusion.4 = f32[512,512]{1,0:T(8,128)} fusion(bf16[1024,512]{1,0:T(8,128)(2,1)S(1)} %bitcast.81, bf16[1024,512]{1,0:T(8,128)(2,1)S(1)} %bitcast.72), kind=kOutput, calls=%fused_computation.47 | convolution fusion | flops 536870912 | bytes 3145728 | tf_op jit(solution)/shard_map/dot_general | solution.py:63
  149.1 1.7 %fusion.3 = f32[512,512]{1,0:T(8,128)} fusion(bf16[1024,512]{1,0:T(8,128)(2,1)S(1)} %bitcast.80, bf16[1024,512]{1,0:T(8,128)(2,1)S(1)} %bitcast.73), kind=kOutput, calls=%fused_computation.46 | convolution fusion | flops 536870912 | bytes 3145728 | tf_op jit(solution)/shard_map/dot_general | solution.py:63
  150.8 2.4 %convolution_add_fusion = f32[512,512]{1,0:T(8,128)S(1)} fusion(f32[512,512]{1,0:T(8,128)} %fusion.4, bf16[1024,512]{1,0:T(8,128)(2,1)} %bitcast.79, bf16[1024,512]{1,0:T(8,128)(2,1)S(1)} %bitcast.74), kind=kOutput, calls=%fused_computation.8 | convolution fusion | flops 537133056 | bytes 4194304 | tf_op jit(solution)/shard_map/dot_general | solution.py:63
  153.1 0.7 convolution_add_fusion.1
  153.9 1.7 %maximum_divide_fusion = f32[1024,512]{1,0:T(8,128)} fusion(f32[512,512]{1,0:T(8,128)S(1)} %convolution_add_fusion, f32[512,512]{1,0:T(8,128)S(1)} %convolution_add_fusion.1, f32[512]{0:T(512)S(1)} %sub.19, f32[1024]{0:T(1024)S(1)} %sub.18), kind=kLoop, calls=%fused_computation | loop fusion | flops 1572864 | bytes 4200448 | tf_op jit(solution)/shard_map/div | solution.py:148
  (48 shorter events, 1.4 us)
Async XLA Ops:
  0.0 51.5 %collective-permute-start = (bf16[1024,512]{1,0:T(8,128)(2,1)}, bf16[1024,512]{1,0:T(8,128)(2,1)S(1)}, u32[]{:S(2)}, u32[]{:S(2)}) collective-permute-start(bf16[1024,512]{1,0:T(8,128)(2,1)} %param.7), channel_id=1, source_target_pairs={{0,1},{1,0},{2,3},{3,2},{4,5},{5,4},{6,7},{7,6},{8,9},{9,8},{10,11... | collective-permute-start | bytes 3145736 | tf_op jit(solution)/shard_map/ppermute | solution.py:97
  49.5 1.2 copy-start
  53.2 5.1 %copy-start.1 = (bf16[512,64]{0,1:T(8,128)(2,1)S(1)}, bf16[512,64]{0,1:T(8,128)(2,1)}, u32[]{:S(2)}) copy-start(bf16[512,64]{0,1:T(8,128)(2,1)} %param.9) | copy-start | bytes 196612
  53.2 7.4 %copy-start.2 = (s32[16384]{0:T(1024)S(1)}, s32[16384]{0:T(1024)}, u32[]{:S(2)}) copy-start(s32[16384]{0:T(1024)} %param.10) | copy-start | bytes 196612
  53.2 14.7 %all-to-all-start = ((f16[4,128,1024]{2,1,0:T(8,128)(2,1)}), f16[4,128,1024]{2,1,0:T(8,128)(2,1)}, u32[]{:S(2)}, u32[]{:S(2)}) async-start(f16[4,128,1024]{2,1,0:T(8,128)(2,1)} %bitcast.11), calls=%async_computation | async-start | bytes 2097152 | tf_op jit(solution)/shard_map/all_to_all | solution.py:106
  58.4 19.7 %collective-permute-start.1 = (f16[64,512]{1,0:T(8,128)(2,1)S(1)}, f16[64,512]{1,0:T(8,128)(2,1)S(1)}, u32[]{:S(2)}, u32[]{:S(2)}) collective-permute-start(f16[64,512]{1,0:T(8,128)(2,1)S(1)} %multiply_convert_fusion.12), channel_id=1, source_target_pairs={{0,0},{1,1},{2,32},{3,33},{4,64},{5,65},{6,96},{7,97},{8,128},{9,1... | collective-permute-start | bytes 196616 | tf_op jit(solution)/shard_map/ppermute | solution.py:105
  60.7 15.7 %copy-start.5 = (f32[64]{0:T(128)S(1)}, f32[64]{0:T(128)}, u32[]{:S(2)}) copy-start(f32[64]{0:T(128)} %param.12) | copy-start | bytes 772
  60.7 15.8 %copy-start.3 = (s32[16384]{0:T(1024)S(1)}, s32[16384]{0:T(1024)}, u32[]{:S(2)}) copy-start(s32[16384]{0:T(1024)} %param.11) | copy-start | bytes 196612
  70.1 13.1 %all-to-all-start.1 = ((f16[4,32,1024]{2,1,0:T(8,128)(2,1)}), f16[4,32,1024]{2,1,0:T(8,128)(2,1)S(1)}, u32[]{:S(2)}, u32[]{:S(2)}) async-start(f16[4,32,1024]{2,1,0:T(8,128)(2,1)} %bitcast.12), calls=%async_computation.1 | async-start | bytes 524288 | tf_op jit(solution)/shard_map/all_to_all | solution.py:109
  76.6 0.7 copy-start.4
  76.6 0.9 dynamic-slice-start.1
  76.6 1.3 dynamic-slice-start
  83.3 26.5 %collective-permute-start.2 = (bf16[32,1024]{1,0:T(8,128)(2,1)S(1)}, bf16[32,1024]{1,0:T(8,128)(2,1)S(1)}, u32[]{:S(2)}, u32[]{:S(2)}) collective-permute-start(bf16[32,1024]{1,0:T(8,128)(2,1)S(1)} %get-tuple-element.27), channel_id=1, source_target_pairs={{0,0},{1,1},{2,32},{3,33},{4,256},{5,257},{6,288},{7,289},{8,64},{... | collective-permute-start | bytes 196616 | tf_op jit(solution)/shard_map/ppermute | solution.py:117
  87.1 22.7 %collective-permute-start.3 = (bf16[32,1024]{1,0:T(8,128)(2,1)S(1)}, bf16[32,1024]{1,0:T(8,128)(2,1)S(1)}, u32[]{:S(2)}, u32[]{:S(2)}) collective-permute-start(bf16[32,1024]{1,0:T(8,128)(2,1)S(1)} %get-tuple-element.27), channel_id=1, source_target_pairs={{0,256},{1,257},{2,288},{3,289},{4,0},{5,1},{6,32},{7,33},{8,320},... | collective-permute-start | bytes 196616 | tf_op jit(solution)/shard_map/ppermute | solution.py:118
  111.2 39.6 %all-to-all-start.2 = ((bf16[16,2,32,512]{3,2,1,0:T(8,128)(2,1)}), bf16[16,2,32,512]{3,2,1,0:T(8,128)(2,1)S(1)}, u32[]{:S(2)}, u32[]{:S(2)}) async-start(bf16[16,2,32,512]{3,2,1,0:T(8,128)(2,1)} %bitcast.29), calls=%async_computation.2 | async-start | bytes 2097152 | tf_op jit(solution)/shard_map/all_to_all | solution.py:131
  150.8 2.4 %copy-start.6 = (f32[512,512]{1,0:T(8,128)S(1)}, f32[512,512]{1,0:T(8,128)}, u32[]{:S(2)}) copy-start(f32[512,512]{1,0:T(8,128)} %fusion.3) | copy-start | bytes 3145732

commit v3 on v2

--- a/solution.py
+++ b/solution.py
@@ -132,13 +132,14 @@
     both = lax.all_gather(both, ("x", "core"), axis=0).reshape(4, 2, 512, cols)
     mirror = mirror.reshape(1024, cols)
 
-    halves = []
-    for half in range(2):
-        right_rows = restore(both[:, half, :256], RIGHT_SCALE).reshape(1024, cols)
-        start = 256 + half * 128
-        fitted_rows = restore(both[:, :, start : start + 128], FIT_SCALE).reshape(1024, cols)
-        halves.append(contract(fitted_rows, right_cols) + contract(right_rows, mirror))
-    total = jnp.concatenate(halves, axis=0)
+    right_rows = jnp.concatenate(
+        [restore(both[:, half, :256], RIGHT_SCALE).reshape(1024, cols) for half in range(2)], axis=1
+    )
+    fitted_rows = both[:, :, 256:].reshape(4, 2, 2, 128, cols)
+    fitted_rows = jnp.concatenate(
+        [restore(fitted_rows[:, :, half], FIT_SCALE).reshape(1024, cols) for half in range(2)], axis=1
+    )
+    total = contract(fitted_rows, right_cols) + contract(right_rows, mirror)
     row_gap = pair_gap(
         occupied_map, virtual_map, occupied_energy, virtual_energy, row_block * rows, rows
     )

time: 158 us -> 157 us (level)
  other arithmetic: 8.57 us -> 6.92 us
    div x1 -> x0, other arithmetic: 1.67 us -> none  [per_device(): return total / (row_gap[:, None] + col_gap[None, :])]
    dot_general x4 -> x2, matrix products: 6.49 us -> 7.13 us  [contract(): lax.dot_general(left, right, (((0,), (0,)), ((), ())), preferred_element_...]
where the time goes in v3:
time: 157 us; the launch traced here: 155 us
  blocking collectives  83.8 us (53%)
  starting transfers between devices  38.6 us (25%)
  waiting for transfers between devices  12.1 us (8%)
  matrix products  9.6 us (6%)
  other arithmetic  6.92 us (4%)
  local copies, waits for them, and re-layouts  3.65 us (2%)
    all_gather x1, blocking collectives, per_device(): factors = lax.all_gather(chunk, 'y', axis=0, tiled=True)  31.6 us
    all_gather x1, blocking collectives, per_device(): both = lax.all_gather(both, ('x', 'core'), axis=0).reshape(4, 2, 512, cols)  21.5 us
    all_gather x1, blocking collectives, per_device(): lax.all_gather(jnp.concatenate([right_moved, light], axis=0), 'zl', axis=0)  15.8 us
    all_gather x1, blocking collectives, per_device(): near = lax.all_gather(pair, ('zh', 'core'), axis=0).reshape(2, 2, 128, cols)  14.8 us
    all_to_all x1, starting transfers between devices, per_device(): lax.all_to_all(mirror.reshape(16, 2, 32, cols), ('y', 'core'), 0, 0)  12.5 us
    dot_general x2, matrix products, contract(): lax.dot_general(left, right, (((0,), (0,)), ((), ())), preferred_element_...  7.13 us
    all_to_all x1, waiting for transfers between devices, per_device(): arrived = lax.all_to_all(sent, 'x', 0, 0)  6.95 us
    ppermute x1, starting transfers between devices, per_device(): cross = lax.ppermute(fitted, ALL, chips(to_column, 1))  6.76 us
  transfers between devices with their start and end apart: 7, of which 2 were waited for; matrix products, arithmetic and copies ran while one was open for 7% of the time, Pallas kernels for 0%

profile of v3, /device:TPU:2, one launch (start us, length us, event | category | flops | bytes accessed | tf_op | source)
XLA Modules:
  0.0 155.0 jit_solution(16237094171315427251)
XLA Ops:
  0.0 1.9 %collective-permute-start = (bf16[1024,512]{1,0:T(8,128)(2,1)}, bf16[1024,512]{1,0:T(8,128)(2,1)S(1)}, u32[]{:S(2)}, u32[]{:S(2)}) collective-permute-start(bf16[1024,512]{1,0:T(8,128)(2,1)} %param.7), channel_id=1, source_target_pairs={{0,1},{1,0},{2,3},{3,2},{4,5},{5,4},{6,7},{7,6},{8,9},{9,8},{10,11... | collective-permute-start | bytes 3145736 | tf_op jit(solution)/shard_map/ppermute | solution.py:97
  1.9 0.9 pad_maximum_fusion.2
  2.8 14.8 %all-gather = bf16[512,512]{1,0:T(8,128)(2,1)S(1)} all-gather(bf16[128,512]{1,0:T(8,128)(2,1)S(1)} %pad_maximum_fusion.2), channel_id=2, replica_groups=mesh['zh'=2,'y'=8,'zl'=4,'x'=4,'core'=2] {'zh','core'}, dimensions={0}, use_global_device_ids=true | all-gather | bytes 655360 | tf_op jit(solution)/shard_map/all_gather | solution.py:77
  17.9 31.6 %all-gather.5 = f16[16,128,512]{2,1,0:T(8,128)(2,1)S(1)} all-gather(f16[2,128,512]{2,1,0:T(8,128)(2,1)S(1)} %pad_maximum_fusion.1), channel_id=1, replica_groups=mesh['zh'=2,'y'=8,'zl'=4,'x'=4,'core'=2] {'y'}, dimensions={0}, use_global_device_ids=true | all-gather | bytes 2359296 | tf_op jit(solution)/shard_map/all_gather | solution.py:90
  49.5 0.3 multiply_convert_fusion.6
  49.9 0.8 copy-done
  50.7 0.7 fusion.14
  51.5 1.7 %multiply_convert_fusion.5 = f16[512,1024]{1,0:T(8,128)(2,1)} fusion(f32[512,1024]{1,0:T(8,128)S(1)} %fusion.14, bf16[512,512]{1,0:T(8,128)(2,1)S(1)} %bitcast.63, bf16[1024,512]{1,0:T(8,128)(2,1)S(1)} %collective-permute-done), kind=kOutput, calls=%fused_computation.15 | convolution fusion | flops 538443776 | bytes 4718592 | tf_op jit(solution)/shard_map/dot_general | solution.py:101
  53.2 5.1 %all-to-all-start = ((f16[4,128,1024]{2,1,0:T(8,128)(2,1)}), f16[4,128,1024]{2,1,0:T(8,128)(2,1)}, u32[]{:S(2)}, u32[]{:S(2)}) async-start(f16[4,128,1024]{2,1,0:T(8,128)(2,1)} %bitcast.11), calls=%async_computation | async-start | bytes 2097152 | tf_op jit(solution)/shard_map/all_to_all | solution.py:106
  58.4 2.2 %collective-permute-start.1 = (f16[64,512]{1,0:T(8,128)(2,1)S(1)}, f16[64,512]{1,0:T(8,128)(2,1)S(1)}, u32[]{:S(2)}, u32[]{:S(2)}) collective-permute-start(f16[64,512]{1,0:T(8,128)(2,1)S(1)} %multiply_convert_fusion.12), channel_id=1, source_target_pairs={{0,0},{1,1},{2,32},{3,33},{4,64},{5,65},{6,96},{7,97},{8,128},{9,1... | collective-permute-start | bytes 196616 | tf_op jit(solution)/shard_map/ppermute | solution.py:105
  60.7 0.2 multiply_convert_fusion.2
  60.9 6.9 %all-to-all-done = f16[4,128,1024]{2,1,0:T(8,128)(2,1)} async-done(((f16[4,128,1024]{2,1,0:T(8,128)(2,1)}), f16[4,128,1024]{2,1,0:T(8,128)(2,1)}, u32[]{:S(2)}, u32[]{:S(2)}) %all-to-all-start) | async-done | bytes 1048608 | tf_op jit(solution)/shard_map/all_to_all | solution.py:106
  67.9 1.5 convert_reduce_fusion
  69.4 0.8 multiply_convert_fusion.8
  70.1 6.3 %all-to-all-start.1 = ((f16[4,32,1024]{2,1,0:T(8,128)(2,1)}), f16[4,32,1024]{2,1,0:T(8,128)(2,1)S(1)}, u32[]{:S(2)}, u32[]{:S(2)}) async-start(f16[4,32,1024]{2,1,0:T(8,128)(2,1)} %bitcast.12), calls=%async_computation.1 | async-start | bytes 524288 | tf_op jit(solution)/shard_map/all_to_all | solution.py:109
  76.8 0.5 copy-done.4
  77.3 0.2 select_reduce_fusion.1
  77.6 0.4 select_reduce_fusion
  77.9 0.1 select_reduce_fusion.2
  78.1 5.1 %all-to-all-done.1 = f16[4,32,1024]{2,1,0:T(8,128)(2,1)S(1)} async-done(((f16[4,32,1024]{2,1,0:T(8,128)(2,1)}), f16[4,32,1024]{2,1,0:T(8,128)(2,1)S(1)}, u32[]{:S(2)}, u32[]{:S(2)}) %all-to-all-start.1) | async-done | bytes 262176 | tf_op jit(solution)/shard_map/all_to_all | solution.py:109
  83.3 3.8 %collective-permute-start.2 = (bf16[32,1024]{1,0:T(8,128)(2,1)S(1)}, bf16[32,1024]{1,0:T(8,128)(2,1)S(1)}, u32[]{:S(2)}, u32[]{:S(2)}) collective-permute-start(bf16[32,1024]{1,0:T(8,128)(2,1)S(1)} %get-tuple-element.27), channel_id=1, source_target_pairs={{0,0},{1,1},{2,32},{3,33},{4,256},{5,257},{6,288},{7,289},{8,64},{... | collective-permute-start | bytes 196616 | tf_op jit(solution)/shard_map/ppermute | solution.py:117
  87.1 6.8 %collective-permute-start.3 = (bf16[32,1024]{1,0:T(8,128)(2,1)S(1)}, bf16[32,1024]{1,0:T(8,128)(2,1)S(1)}, u32[]{:S(2)}, u32[]{:S(2)}) collective-permute-start(bf16[32,1024]{1,0:T(8,128)(2,1)S(1)} %get-tuple-element.27), channel_id=1, source_target_pairs={{0,256},{1,257},{2,288},{3,289},{4,0},{5,1},{6,32},{7,33},{8,320},... | collective-permute-start | bytes 196616 | tf_op jit(solution)/shard_map/ppermute | solution.py:118
  94.0 15.8 %all-gather.1 = f16[512,512]{1,0:T(8,128)(2,1)S(1)} all-gather(f16[128,512]{1,0:T(8,128)(2,1)S(1)} %pad_maximum_fusion.3), channel_id=3, replica_groups=mesh['zh'=2,'y'=8,'zl'=4,'x'=4,'core'=2] {'zl'}, dimensions={0}, use_global_device_ids=true | all-gather | bytes 655360 | tf_op jit(solution)/shard_map/all_gather | solution.py:119
  110.1 1.1 broadcast_in_dim.68
  111.2 12.5 %all-to-all-start.2 = ((bf16[16,2,32,512]{3,2,1,0:T(8,128)(2,1)}), bf16[16,2,32,512]{3,2,1,0:T(8,128)(2,1)S(1)}, u32[]{:S(2)}, u32[]{:S(2)}) async-start(bf16[16,2,32,512]{3,2,1,0:T(8,128)(2,1)} %bitcast.32), calls=%async_computation.2 | async-start | bytes 2097152 | tf_op jit(solution)/shard_map/all_to_all | solution.py:131
  123.7 0.1 pad_maximum_fusion
  123.8 21.5 %all-gather.6 = f16[4096,512]{1,0:T(8,128)(2,1)S(1)} all-gather(f16[512,512]{1,0:T(8,128)(2,1)S(1)} %pad_maximum_fusion), channel_id=4, replica_groups=mesh['zh'=2,'y'=8,'zl'=4,'x'=4,'core'=2] {'x','core'}, dimensions={0}, use_global_device_ids=true | all-gather | bytes 4718592 | tf_op jit(solution)/shard_map/all_gather | solution.py:132
  145.3 0.5 slice.75
  145.8 1.5 multiply_convert_fusion.1
  147.3 0.5 multiply_convert_fusion.4
  147.9 2.6 %fusion = f32[1024,512]{1,0:T(8,128)} fusion(bf16[1024,512]{1,0:T(8,128)(2,1)S(1)} %bitcast.68, bf16[1024,512]{1,0:T(8,128)(2,1)S(1)} %bitcast.75, bf16[1024,512]{1,0:T(8,128)(2,1)S(1)} %bitcast.74), kind=kOutput, calls=%fused_computation | convolution fusion | flops 1077936128 | bytes 5242880 | tf_op jit(solution)/shard_map/dot_general | solution.py:63
  150.5 4.5 %add_divide_fusion = f32[1024,512]{1,0:T(8,128)} fusion(f32[1024,512]{1,0:T(8,128)} %fusion, bf16[1024,512]{1,0:T(8,128)(2,1)S(1)} %bitcast.69, bf16[1024,512]{1,0:T(8,128)(2,1)} %bitcast.73, bf16[1024,512]{1,0:T(8,128)(2,1)S(1)} %bitcast.72, f32[512]{0:T(512)S(1)} %sub.19, f32[1024]{0:T(1024)S(1)} %sub.18), kind=kOutput, calls=%fused_computation.8 | convolution fusion | flops 1079508992 | bytes 7346176 | tf_op jit(solution)/shard_map/dot_general | solution.py:63
  (44 shorter events, 1.1 us)
Async XLA Ops:
  0.0 51.5 %collective-permute-start = (bf16[1024,512]{1,0:T(8,128)(2,1)}, bf16[1024,512]{1,0:T(8,128)(2,1)S(1)}, u32[]{:S(2)}, u32[]{:S(2)}) collective-permute-start(bf16[1024,512]{1,0:T(8,128)(2,1)} %param.7), channel_id=1, source_target_pairs={{0,1},{1,0},{2,3},{3,2},{4,5},{5,4},{6,7},{7,6},{8,9},{9,8},{10,11... | collective-permute-start | bytes 3145736 | tf_op jit(solution)/shard_map/ppermute | solution.py:97
  49.5 1.2 copy-start
  53.2 5.1 %copy-start.1 = (bf16[512,64]{0,1:T(8,128)(2,1)S(1)}, bf16[512,64]{0,1:T(8,128)(2,1)}, u32[]{:S(2)}) copy-start(bf16[512,64]{0,1:T(8,128)(2,1)} %param.9) | copy-start | bytes 196612
  53.2 7.4 %copy-start.2 = (s32[16384]{0:T(1024)S(1)}, s32[16384]{0:T(1024)}, u32[]{:S(2)}) copy-start(s32[16384]{0:T(1024)} %param.10) | copy-start | bytes 196612
  53.2 14.7 %all-to-all-start = ((f16[4,128,1024]{2,1,0:T(8,128)(2,1)}), f16[4,128,1024]{2,1,0:T(8,128)(2,1)}, u32[]{:S(2)}, u32[]{:S(2)}) async-start(f16[4,128,1024]{2,1,0:T(8,128)(2,1)} %bitcast.11), calls=%async_computation | async-start | bytes 2097152 | tf_op jit(solution)/shard_map/all_to_all | solution.py:106
  58.4 19.7 %collective-permute-start.1 = (f16[64,512]{1,0:T(8,128)(2,1)S(1)}, f16[64,512]{1,0:T(8,128)(2,1)S(1)}, u32[]{:S(2)}, u32[]{:S(2)}) collective-permute-start(f16[64,512]{1,0:T(8,128)(2,1)S(1)} %multiply_convert_fusion.12), channel_id=1, source_target_pairs={{0,0},{1,1},{2,32},{3,33},{4,64},{5,65},{6,96},{7,97},{8,128},{9,1... | collective-permute-start | bytes 196616 | tf_op jit(solution)/shard_map/ppermute | solution.py:105
  60.7 15.7 %copy-start.5 = (f32[64]{0:T(128)S(1)}, f32[64]{0:T(128)}, u32[]{:S(2)}) copy-start(f32[64]{0:T(128)} %param.12) | copy-start | bytes 772
  60.7 15.8 %copy-start.3 = (s32[16384]{0:T(1024)S(1)}, s32[16384]{0:T(1024)}, u32[]{:S(2)}) copy-start(s32[16384]{0:T(1024)} %param.11) | copy-start | bytes 196612
  70.1 13.1 %all-to-all-start.1 = ((f16[4,32,1024]{2,1,0:T(8,128)(2,1)}), f16[4,32,1024]{2,1,0:T(8,128)(2,1)S(1)}, u32[]{:S(2)}, u32[]{:S(2)}) async-start(f16[4,32,1024]{2,1,0:T(8,128)(2,1)} %bitcast.12), calls=%async_computation.1 | async-start | bytes 524288 | tf_op jit(solution)/shard_map/all_to_all | solution.py:109
  76.6 0.7 copy-start.4
  76.6 0.9 dynamic-slice-start.1
  76.6 1.3 dynamic-slice-start
  83.3 26.5 %collective-permute-start.2 = (bf16[32,1024]{1,0:T(8,128)(2,1)S(1)}, bf16[32,1024]{1,0:T(8,128)(2,1)S(1)}, u32[]{:S(2)}, u32[]{:S(2)}) collective-permute-start(bf16[32,1024]{1,0:T(8,128)(2,1)S(1)} %get-tuple-element.27), channel_id=1, source_target_pairs={{0,0},{1,1},{2,32},{3,33},{4,256},{5,257},{6,288},{7,289},{8,64},{... | collective-permute-start | bytes 196616 | tf_op jit(solution)/shard_map/ppermute | solution.py:117
  87.1 22.7 %collective-permute-start.3 = (bf16[32,1024]{1,0:T(8,128)(2,1)S(1)}, bf16[32,1024]{1,0:T(8,128)(2,1)S(1)}, u32[]{:S(2)}, u32[]{:S(2)}) collective-permute-start(bf16[32,1024]{1,0:T(8,128)(2,1)S(1)} %get-tuple-element.27), channel_id=1, source_target_pairs={{0,256},{1,257},{2,288},{3,289},{4,0},{5,1},{6,32},{7,33},{8,320},... | collective-permute-start | bytes 196616 | tf_op jit(solution)/shard_map/ppermute | solution.py:118
  111.2 39.3 %all-to-all-start.2 = ((bf16[16,2,32,512]{3,2,1,0:T(8,128)(2,1)}), bf16[16,2,32,512]{3,2,1,0:T(8,128)(2,1)S(1)}, u32[]{:S(2)}, u32[]{:S(2)}) async-start(bf16[16,2,32,512]{3,2,1,0:T(8,128)(2,1)} %bitcast.32), calls=%async_computation.2 | async-start | bytes 2097152 | tf_op jit(solution)/shard_map/all_to_all | solution.py:131

commit v4 on v3

--- a/solution.py
+++ b/solution.py
@@ -73,8 +73,7 @@
     row_block = lax.axis_index(ROW)
     col_block = lax.axis_index(COL + ("core",))
 
-    pair = jnp.concatenate([aux_left.T, aux_right.T], axis=0)
-    near = lax.all_gather(pair, ("zh", "core"), axis=0).reshape(2, 2, 128, cols)
+    near = lax.all_gather(aux_left.T, ("zh", "core"), axis=0).reshape(2, 2, 64, cols)
     mine = lax.dynamic_index_in_dim(near, core, 1, keepdims=False)
     theirs = lax.dynamic_index_in_dim(near, 1 - core, 1, keepdims=False)
     left_near = jnp.concatenate(
@@ -85,15 +84,17 @@
         axis=1,
     )
     chunk = jnp.concatenate(
-        [pack(left_near, LEFT_SCALE), pack(mine[:, 64:], RIGHT_SCALE)], axis=1
+        [
+            pack(left_near, LEFT_SCALE).reshape(128, cols),
+            pack(aux_right.T, RIGHT_SCALE),
+        ],
+        axis=0,
     )
-    factors = lax.all_gather(chunk, "y", axis=0, tiled=True)
-    factors = factors.reshape(2, 2, 2, 2, 128, cols)
-    by_slot = factors.transpose(3, 2, 0, 1, 4, 5)
+    factors = lax.all_gather(chunk, "y", axis=0)
+    by_slot = factors[:, :128].reshape(2, 2, 2, 2, 64, cols).transpose(3, 2, 0, 1, 4, 5)
     left_kept = restore(by_slot[..., :32, :], LEFT_SCALE).reshape(512, cols)
     left_taken = restore(by_slot[..., 32:64, :], LEFT_SCALE).reshape(512, cols)
-    right_cols = by_slot[..., 64:, :].reshape(4, 4, 2, 32, cols).transpose(0, 2, 1, 3, 4)
-    right_cols = restore(right_cols, RIGHT_SCALE).reshape(1024, cols)
+    right_near = restore(factors[:, 128:], RIGHT_SCALE).reshape(512, cols)
     other_amplitudes = lax.ppermute(amplitudes, "core", SWAP)
 
     partial = lax.dot_general(
@@ -104,6 +105,7 @@
     sent = (partial * SUM_SCALE).astype(jnp.float16).reshape(4, 128, rows)
     right_moved = lax.ppermute(pack(aux_right.T, RIGHT_SCALE), ALL, chips(to_row))
     arrived = lax.all_to_all(sent, "x", 0, 0)
+    low = lax.axis_index("zh") == 0
     summed = jnp.sum(arrived.astype(jnp.float32), axis=0) * (LINE_SCALE / SUM_SCALE)
     sent = summed.astype(jnp.float16).reshape(4, 32, rows)
     arrived = lax.all_to_all(sent, "zl", 0, 0)
@@ -129,6 +131,7 @@
     )
     mirror = jnp.broadcast_to(mirror_chunk[None], (8,) + mirror_chunk.shape)
     mirror = lax.all_to_all(mirror.reshape(16, 2, 32, cols), ("y", "core"), 0, 0)
+    right_far = lax.ppermute(right_near, "zh", SWAP)
     both = lax.all_gather(both, ("x", "core"), axis=0).reshape(4, 2, 512, cols)
     mirror = mirror.reshape(1024, cols)
 
@@ -139,6 +142,11 @@
     fitted_rows = jnp.concatenate(
         [restore(fitted_rows[:, :, half], FIT_SCALE).reshape(1024, cols) for half in range(2)], axis=1
     )
+    right_cols = jnp.stack(
+        [jnp.where(low, right_near, right_far), jnp.where(low, right_far, right_near)]
+    )
+    right_cols = right_cols.reshape(2, 2, 2, 2, 2, 32, cols).transpose(0, 3, 4, 1, 2, 5, 6)
+    right_cols = right_cols.reshape(1024, cols)
     total = contract(fitted_rows, right_cols) + contract(right_rows, mirror)
     row_gap = pair_gap(
         occupied_map, virtual_map, occupied_energy, virtual_energy, row_block * rows, rows

time: 157 us -> 171 us (1.089)
  the two profiles are of different devices: /device:TPU:2 before, /device:TPU:1 now
where the time goes in v4:
time: 171 us; the launch traced here: 170 us
  blocking collectives  75.3 us (44%)
  starting transfers between devices  47.9 us (28%)
  waiting for transfers between devices  25.6 us (15%)
  matrix products  9.6 us (6%)
  local copies, waits for them, and re-layouts  6.01 us (4%)
  other arithmetic  5.67 us (3%)
    all_gather x1, blocking collectives, per_device(): both = lax.all_gather(both, ('x', 'core'), axis=0).reshape(4, 2, 512, cols)  24.4 us
    all_gather x1, blocking collectives, per_device(): factors = lax.all_gather(chunk, 'y', axis=0)  24 us
    all_gather x1, blocking collectives, per_device(): lax.all_gather(jnp.concatenate([right_moved, light], axis=0), 'zl', axis=0)  16.9 us
    all_to_all x1, waiting for transfers between devices, per_device(): arrived = lax.all_to_all(sent, 'zl', 0, 0)  15.1 us
    all_to_all x1, starting transfers between devices, per_device(): lax.all_to_all(mirror.reshape(16, 2, 32, cols), ('y', 'core'), 0, 0)  12.2 us
    ppermute x1, waiting for transfers between devices, per_device(): right_far = lax.ppermute(right_near, 'zh', SWAP)  10.4 us
    all_gather x1, blocking collectives, per_device(): lax.all_gather(aux_left.T, ('zh', 'core'), axis=0).reshape(2, 2, 64, cols)  9.97 us
    ppermute x1, starting transfers between devices, per_device(): right_far = lax.ppermute(right_near, 'zh', SWAP)  9.68 us
  transfers between devices with their start and end apart: 8, of which 2 were waited for; matrix products, arithmetic and copies ran while one was open for 8% of the time, Pallas kernels for 0%

profile of v4, /device:TPU:1, one launch (start us, length us, event | category | flops | bytes accessed | tf_op | source)
XLA Modules:
  0.0 170.4 jit_solution(15094663560906416690)
XLA Ops:
  0.0 8.7 %collective-permute-start = (bf16[1024,512]{1,0:T(8,128)(2,1)}, bf16[1024,512]{1,0:T(8,128)(2,1)S(1)}, u32[]{:S(2)}, u32[]{:S(2)}) collective-permute-start(bf16[1024,512]{1,0:T(8,128)(2,1)} %param.7), channel_id=1, source_target_pairs={{0,1},{1,0},{2,3},{3,2},{4,5},{5,4},{6,7},{7,6},{8,9},{9,8},{10,11... | collective-permute-start | bytes 3145736 | tf_op jit(solution)/shard_map/ppermute | solution.py:98
  8.7 0.9 fusion.11
  9.6 10.0 %all-gather = bf16[256,512]{1,0:T(8,128)(2,1)S(1)} all-gather(bf16[64,512]{1,0:T(8,128)(2,1)} %bitcast.78), channel_id=2, replica_groups=mesh['zh'=2,'y'=8,'zl'=4,'x'=4,'core'=2] {'zh','core'}, dimensions={0}, use_global_device_ids=true | all-gather | bytes 327680 | tf_op jit(solution)/shard_map/all_gather | solution.py:76
  19.7 24.0 %all-gather.6 = f16[1536,512]{1,0:T(8,128)(2,1)S(1)} all-gather(f16[192,512]{1,0:T(8,128)(2,1)S(1)} %pad_maximum_fusion.1), channel_id=3, replica_groups=mesh['zh'=2,'y'=8,'zl'=4,'x'=4,'core'=2] {'y'}, dimensions={0}, use_global_device_ids=true | all-gather | bytes 1769472 | tf_op jit(solution)/shard_map/all_gather | solution.py:93
  44.0 0.3 multiply_convert_fusion.6
  44.4 0.8 copy-done
  45.2 0.7 fusion.15
  46.0 1.7 %multiply_convert_fusion.4 = f16[512,1024]{1,0:T(8,128)(2,1)} fusion(f32[512,1024]{1,0:T(8,128)S(1)} %fusion.15, bf16[512,512]{1,0:T(8,128)(2,1)S(1)} %bitcast.63, bf16[1024,512]{1,0:T(8,128)(2,1)S(1)} %collective-permute-done), kind=kOutput, calls=%fused_computation.14 | convolution fusion | flops 538443776 | bytes 4718592 | tf_op jit(solution)/shard_map/dot_general | solution.py:102
  47.7 3.6 %all-to-all-start = ((f16[4,128,1024]{2,1,0:T(8,128)(2,1)}), f16[4,128,1024]{2,1,0:T(8,128)(2,1)S(1)}, u32[]{:S(2)}, u32[]{:S(2)}) async-start(f16[4,128,1024]{2,1,0:T(8,128)(2,1)} %bitcast.61), calls=%async_computation | async-start | bytes 2097152 | tf_op jit(solution)/shard_map/all_to_all | solution.py:107
  51.4 0.7 collective-permute-start.1
  52.1 9.7 %collective-permute-start.4 = (bf16[512,512]{1,0:T(8,128)(2,1)S(1)}, bf16[512,512]{1,0:T(8,128)(2,1)S(1)}, u32[]{:S(2)}, u32[]{:S(2)}) collective-permute-start(bf16[512,512]{1,0:T(8,128)(2,1)S(1)} %bitcast.62), channel_id=1, source_target_pairs={{0,256},{256,0},{1,257},{257,1},{2,258},{258,2},{3,259},{259,3},{4... | collective-permute-start | bytes 1572872 | tf_op jit(solution)/shard_map/ppermute | solution.py:134
  61.8 0.8 dynamic_slice.31
  62.6 0.8 dynamic_slice.32
  63.4 0.7 dynamic_slice.29
  64.1 0.7 dynamic_slice.30
  65.1 0.4 select_reduce_fusion
  65.6 0.2 convert_reduce_fusion
  65.8 0.8 multiply_convert_fusion.8
  66.6 6.5 %all-to-all-start.1 = ((f16[4,32,1024]{2,1,0:T(8,128)(2,1)}), f16[4,32,1024]{2,1,0:T(8,128)(2,1)S(1)}, u32[]{:S(2)}, u32[]{:S(2)}) async-start(f16[4,32,1024]{2,1,0:T(8,128)(2,1)} %bitcast.13), calls=%async_computation.1 | async-start | bytes 524288 | tf_op jit(solution)/shard_map/all_to_all | solution.py:111
  73.1 10.4 %collective-permute-done.4 = bf16[512,512]{1,0:T(8,128)(2,1)S(1)} collective-permute-done((bf16[512,512]{1,0:T(8,128)(2,1)S(1)}, bf16[512,512]{1,0:T(8,128)(2,1)S(1)}, u32[]{:S(2)}, u32[]{:S(2)}) %collective-permute-start.4) | collective-permute-done | bytes 524320 | tf_op jit(solution)/shard_map/ppermute | solution.py:134
  83.9 15.1 %all-to-all-done.1 = f16[4,32,1024]{2,1,0:T(8,128)(2,1)S(1)} async-done(((f16[4,32,1024]{2,1,0:T(8,128)(2,1)}), f16[4,32,1024]{2,1,0:T(8,128)(2,1)S(1)}, u32[]{:S(2)}, u32[]{:S(2)}) %all-to-all-start.1) | async-done | bytes 262176 | tf_op jit(solution)/shard_map/all_to_all | solution.py:111
  99.1 0.7 collective-permute-start.2
  99.7 5.8 %collective-permute-start.3 = (bf16[32,1024]{1,0:T(8,128)(2,1)S(1)}, bf16[32,1024]{1,0:T(8,128)(2,1)S(1)}, u32[]{:S(2)}, u32[]{:S(2)}) collective-permute-start(bf16[32,1024]{1,0:T(8,128)(2,1)S(1)} %get-tuple-element.29), channel_id=1, source_target_pairs={{0,256},{1,257},{2,288},{3,289},{4,0},{5,1},{6,32},{7,33},{8,320},... | collective-permute-start | bytes 196616 | tf_op jit(solution)/shard_map/ppermute | solution.py:120
  105.6 16.9 %all-gather.2 = f16[512,512]{1,0:T(8,128)(2,1)S(1)} all-gather(f16[128,512]{1,0:T(8,128)(2,1)S(1)} %pad_maximum_fusion.2), channel_id=4, replica_groups=mesh['zh'=2,'y'=8,'zl'=4,'x'=4,'core'=2] {'zl'}, dimensions={0}, use_global_device_ids=true | all-gather | bytes 655360 | tf_op jit(solution)/shard_map/all_gather | solution.py:121
  122.8 1.1 broadcast_in_dim.68
  123.9 12.2 %all-to-all-start.2 = ((bf16[16,2,32,512]{3,2,1,0:T(8,128)(2,1)}), bf16[16,2,32,512]{3,2,1,0:T(8,128)(2,1)S(1)}, u32[]{:S(2)}, u32[]{:S(2)}) async-start(bf16[16,2,32,512]{3,2,1,0:T(8,128)(2,1)} %bitcast.35), calls=%async_computation.2 | async-start | bytes 2097152 | tf_op jit(solution)/shard_map/all_to_all | solution.py:133
  136.3 24.4 %all-gather.7 = f16[4096,512]{1,0:T(8,128)(2,1)S(1)} all-gather(f16[512,512]{1,0:T(8,128)(2,1)S(1)} %pad_maximum_fusion), channel_id=5, replica_groups=mesh['zh'=2,'y'=8,'zl'=4,'x'=4,'core'=2] {'x','core'}, dimensions={0}, use_global_device_ids=true | all-gather | bytes 4718592 | tf_op jit(solution)/shard_map/all_gather | solution.py:135
  160.7 0.5 slice.75
  161.2 1.6 multiply_convert_fusion.1
  162.7 0.5 multiply_convert_fusion.3
  163.3 2.6 %fusion = f32[1024,512]{1,0:T(8,128)} fusion(bf16[1024,512]{1,0:T(8,128)(2,1)S(1)} %bitcast.68, bf16[1024,512]{1,0:T(8,128)(2,1)S(1)} %bitcast.75, bf16[1024,512]{1,0:T(8,128)(2,1)S(1)} %bitcast.74), kind=kOutput, calls=%fused_computation | convolution fusion | flops 1077936128 | bytes 5242880 | tf_op jit(solution)/shard_map/dot_general | solution.py:63
  165.9 4.5 %add_divide_fusion = f32[1024,512]{1,0:T(8,128)} fusion(f32[1024,512]{1,0:T(8,128)} %fusion, bf16[1024,512]{1,0:T(8,128)(2,1)S(1)} %bitcast.69, bf16[1024,512]{1,0:T(8,128)(2,1)} %bitcast.73, bf16[1024,512]{1,0:T(8,128)(2,1)S(1)} %bitcast.72, f32[512]{0:T(512)S(1)} %sub.19, f32[1024]{0:T(1024)S(1)} %sub.18), kind=kOutput, calls=%fused_computation.8 | convolution fusion | flops 1079508992 | bytes 7346176 | tf_op jit(solution)/shard_map/dot_general | solution.py:63
  (37 shorter events, 1.8 us)
Async XLA Ops:
  0.0 46.0 %collective-permute-start = (bf16[1024,512]{1,0:T(8,128)(2,1)}, bf16[1024,512]{1,0:T(8,128)(2,1)S(1)}, u32[]{:S(2)}, u32[]{:S(2)}) collective-permute-start(bf16[1024,512]{1,0:T(8,128)(2,1)} %param.7), channel_id=1, source_target_pairs={{0,1},{1,0},{2,3},{3,2},{4,5},{5,4},{6,7},{7,6},{8,9},{9,8},{10,11... | collective-permute-start | bytes 3145736 | tf_op jit(solution)/shard_map/ppermute | solution.py:98
  44.0 1.2 copy-start
  47.7 17.0 %copy-start.2 = (f32[64]{0:T(128)S(1)}, f32[64]{0:T(128)}, u32[]{:S(2)}) copy-start(f32[64]{0:T(128)} %param.12) | copy-start | bytes 772
  47.7 17.1 %copy-start.1 = (f32[256]{0:T(256)S(1)}, f32[256]{0:T(256)}, u32[]{:S(2)}) copy-start(f32[256]{0:T(256)} %param.13) | copy-start | bytes 3076
  47.7 17.9 %all-to-all-start = ((f16[4,128,1024]{2,1,0:T(8,128)(2,1)}), f16[4,128,1024]{2,1,0:T(8,128)(2,1)S(1)}, u32[]{:S(2)}, u32[]{:S(2)}) async-start(f16[4,128,1024]{2,1,0:T(8,128)(2,1)} %bitcast.61), calls=%async_computation | async-start | bytes 2097152 | tf_op jit(solution)/shard_map/all_to_all | solution.py:107
  51.4 32.5 %collective-permute-start.1 = (f16[64,512]{1,0:T(8,128)(2,1)S(1)}, f16[64,512]{1,0:T(8,128)(2,1)S(1)}, u32[]{:S(2)}, u32[]{:S(2)}) collective-permute-start(f16[64,512]{1,0:T(8,128)(2,1)S(1)} %fusion.11), channel_id=1, source_target_pairs={{0,0},{1,1},{2,32},{3,33},{4,64},{5,65},{6,96},{7,97},{8,128},{9,1... | collective-permute-start | bytes 196616 | tf_op jit(solution)/shard_map/ppermute | solution.py:106
  52.1 31.4 %collective-permute-start.4 = (bf16[512,512]{1,0:T(8,128)(2,1)S(1)}, bf16[512,512]{1,0:T(8,128)(2,1)S(1)}, u32[]{:S(2)}, u32[]{:S(2)}) collective-permute-start(bf16[512,512]{1,0:T(8,128)(2,1)S(1)} %bitcast.62), channel_id=1, source_target_pairs={{0,256},{256,0},{1,257},{257,1},{2,258},{258,2},{3,259},{259,3},{4... | collective-permute-start | bytes 1572872 | tf_op jit(solution)/shard_map/ppermute | solution.py:134
  66.6 32.4 %all-to-all-start.1 = ((f16[4,32,1024]{2,1,0:T(8,128)(2,1)}), f16[4,32,1024]{2,1,0:T(8,128)(2,1)S(1)}, u32[]{:S(2)}, u32[]{:S(2)}) async-start(f16[4,32,1024]{2,1,0:T(8,128)(2,1)} %bitcast.13), calls=%async_computation.1 | async-start | bytes 524288 | tf_op jit(solution)/shard_map/all_to_all | solution.py:111
  99.1 23.5 %collective-permute-start.2 = (bf16[32,1024]{1,0:T(8,128)(2,1)S(1)}, bf16[32,1024]{1,0:T(8,128)(2,1)S(1)}, u32[]{:S(2)}, u32[]{:S(2)}) collective-permute-start(bf16[32,1024]{1,0:T(8,128)(2,1)S(1)} %get-tuple-element.29), channel_id=1, source_target_pairs={{0,0},{1,1},{2,32},{3,33},{4,256},{5,257},{6,288},{7,289},{8,64},{... | collective-permute-start | bytes 196616 | tf_op jit(solution)/shard_map/ppermute | solution.py:119
  99.7 22.8 %collective-permute-start.3 = (bf16[32,1024]{1,0:T(8,128)(2,1)S(1)}, bf16[32,1024]{1,0:T(8,128)(2,1)S(1)}, u32[]{:S(2)}, u32[]{:S(2)}) collective-permute-start(bf16[32,1024]{1,0:T(8,128)(2,1)S(1)} %get-tuple-element.29), channel_id=1, source_target_pairs={{0,256},{1,257},{2,288},{3,289},{4,0},{5,1},{6,32},{7,33},{8,320},... | collective-permute-start | bytes 196616 | tf_op jit(solution)/shard_map/ppermute | solution.py:120
  123.9 41.9 %all-to-all-start.2 = ((bf16[16,2,32,512]{3,2,1,0:T(8,128)(2,1)}), bf16[16,2,32,512]{3,2,1,0:T(8,128)(2,1)S(1)}, u32[]{:S(2)}, u32[]{:S(2)}) async-start(bf16[16,2,32,512]{3,2,1,0:T(8,128)(2,1)} %bitcast.35), calls=%async_computation.2 | async-start | bytes 2097152 | tf_op jit(solution)/shard_map/all_to_all | solution.py:133
